TPU v7x, 32 devices: a whole 2x2x4 slice. The times are simulated.
32 devices in a mesh: dp: 16 (over z, y, x), seq: 2 (over core).
Axes of the slice: x: 2, y: 2, z: 4, core: 2. Of those that a mesh axis runs over, the one named last changes fastest.
Arguments:
- tokens: bfloat16 [48, 512, 768], P('dp', 'seq'), may hold values from -6 to 6
- prev_logits: bfloat16 [48, 12, 512, 512], P('dp', None, 'seq'), may hold values from -6 to 6
- segment_ids: int32 [48, 512], P('dp'), may hold values from 0 to 5, never falling along the last dimension, each value on 1 to 192 neighbouring positions
- out_cotangent: bfloat16 [48, 512, 768], P('dp', 'seq'), may hold values from -6 to 6
- logit_cotangent: bfloat16 [48, 12, 512, 512], P('dp', None, 'seq'), may hold values from -0.59765625 to 0.59765625
- querymap: bfloat16 [768, 768], P(('dp', 'seq')), may hold values from -0.21875 to 0.21875
- querybias: bfloat16 [768], P(('dp', 'seq')), may hold values from -3 to 3
- keymap: bfloat16 [768, 768], P(('dp', 'seq')), may hold values from -0.21875 to 0.21875
- valuemap: bfloat16 [768, 768], P(('dp', 'seq')), may hold values from -0.21875 to 0.21875
- valuebias: bfloat16 [768], P(('dp', 'seq')), may hold values from -3 to 3
- mixmap: bfloat16 [768, 768], P(('dp', 'seq')), may hold values from -1.75 to 1.75
- mixbias: bfloat16 [768], P(('dp', 'seq')), may hold values from -3 to 3
- normgain: bfloat16 [768], P(('dp', 'seq')), may hold values from 0.5 to 1.5
- normbias: bfloat16 [768], P(('dp', 'seq')), may hold values from -3 to 3
- expandmap: bfloat16 [768, 3072], P(('dp', 'seq')), may hold values from -0.21875 to 0.21875
- expandbias: bfloat16 [3072], P(('dp', 'seq')), may hold values from -3 to 3
- shrinkmap: bfloat16 [3072, 768], P(('dp', 'seq')), may hold values from -0.109375 to 0.109375
- shrinkbias: bfloat16 [768], P(('dp', 'seq')), may hold values from -3 to 3
- outgain: bfloat16 [768], P(('dp', 'seq')), may hold values from 0.5 to 1.5
- outbias: bfloat16 [768], P(('dp', 'seq')), may hold values from -3 to 3
Outputs:
- layer_out: bfloat16 [48, 512, 768], P('dp', 'seq')
- raw_logits: bfloat16 [48, 12, 512, 512], P('dp', None, 'seq')
- tokens_grad: bfloat16 [48, 512, 768], P('dp', 'seq')
- logits_grad: bfloat16 [48, 12, 512, 512], P('dp', None, 'seq')
- querymap_grad: float32 [768, 768], P(('dp', 'seq'))
- querybias_grad: float32 [768], P(('dp', 'seq'))
- keymap_grad: float32 [768, 768], P(('dp', 'seq'))
- valuemap_grad: float32 [768, 768], P(('dp', 'seq'))
- valuebias_grad: float32 [768], P(('dp', 'seq'))
- mixmap_grad: float32 [768, 768], P(('dp', 'seq'))
- mixbias_grad: float32 [768], P(('dp', 'seq'))
- normgain_grad: float32 [768], P(('dp', 'seq'))
- normbias_grad: float32 [768], P(('dp', 'seq'))
- expandmap_grad: float32 [768, 3072], P(('dp', 'seq'))
- expandbias_grad: float32 [3072], P(('dp', 'seq'))
- shrinkmap_grad: float32 [3072, 768], P(('dp', 'seq'))
- shrinkbias_grad: float32 [768], P(('dp', 'seq'))
- outgain_grad: float32 [768], P(('dp', 'seq'))
- outbias_grad: float32 [768], P(('dp', 'seq'))
Inputs may be any that keep to these rules, and one draw needn't show every extreme that they name: `segment_ids`: along each row the ids never fall; each id covers 1 to 192 slots and in each row one covers exactly that many.
All inputs are finite; a program needn't handle non-finite values.
Results may differ from a plain program's by a relative error of at most 0.014.
Values may be sent and summed in bfloat16 or wider, within the bound.
A program may use at most 192 MiB of HBM per device.

v0:
```python
from functools import partial

import jax
import jax.numpy as jnp
from jax import lax
from jax.sharding import PartitionSpec as P

H = 12
HD = 64


norm_eps = 1e-06
mask_fill = -1e30


def matmul(left_side, right_side):
    return jnp.dot(left_side, right_side, preferred_element_type=jnp.float32)


def rows_product(left_side, right_side):
    return lax.dot_general(
        left_side, right_side, (((0,), (0,)), ((), ())), preferred_element_type=jnp.float32
    )


def cols_product(left_side, right_side):
    return lax.dot_general(
        left_side, right_side, (((1,), (1,)), ((), ())), preferred_element_type=jnp.float32
    )


def column_sum(matrix):
    return jnp.sum(matrix.astype(jnp.float32), 0)


def normalize(hidden):
    center = hidden - jnp.mean(hidden, -1, keepdims=True)
    scaled = lax.rsqrt(jnp.mean(center * center, -1, keepdims=True) + norm_eps)
    return (center * scaled, scaled)


def norm_back(upstream, unit_rows, scaled, gain_row):
    pulled = upstream * gain_row
    return scaled * (
        pulled
        - jnp.mean(pulled, -1, keepdims=True)
        - unit_rows * jnp.mean(pulled * unit_rows, -1, keepdims=True)
    )


def forward(shards, tokens, prev_logits, same_segment):
    (
        querymap,
        querybias,
        keymap,
        valuemap,
        valuebias,
        mixmap,
        mixbias,
        normgain,
        normbias,
        expandmap,
        expandbias,
        shrinkmap,
        shrinkbias,
        outgain,
        outbias,
    ) = shards
    weights = (
        lax.all_gather(querymap, ("dp", "seq"), axis=0, tiled=True),
        lax.all_gather(querybias, ("dp", "seq"), axis=0, tiled=True),
        lax.all_gather(keymap, ("dp", "seq"), axis=0, tiled=True),
        lax.all_gather(valuemap, ("dp", "seq"), axis=0, tiled=True),
        lax.all_gather(valuebias, ("dp", "seq"), axis=0, tiled=True),
        lax.all_gather(mixmap, ("dp", "seq"), axis=0, tiled=True),
        lax.all_gather(mixbias, ("dp", "seq"), axis=0, tiled=True),
        lax.all_gather(normgain, ("dp", "seq"), axis=0, tiled=True),
        lax.all_gather(normbias, ("dp", "seq"), axis=0, tiled=True),
        lax.all_gather(expandmap, ("dp", "seq"), axis=0, tiled=True),
        lax.all_gather(expandbias, ("dp", "seq"), axis=0, tiled=True),
        lax.all_gather(shrinkmap, ("dp", "seq"), axis=0, tiled=True),
        lax.all_gather(shrinkbias, ("dp", "seq"), axis=0, tiled=True),
        lax.all_gather(outgain, ("dp", "seq"), axis=0, tiled=True),
        lax.all_gather(outbias, ("dp", "seq"), axis=0, tiled=True),
    )
    (
        querymap,
        querybias,
        keymap,
        valuemap,
        valuebias,
        mixmap,
        mixbias,
        normgain,
        normbias,
        expandmap,
        expandbias,
        shrinkmap,
        shrinkbias,
        outgain,
        outbias,
    ) = weights
    seqrows, qlength, width = tokens.shape
    klength = prev_logits.shape[3]
    factor = HD ** (-0.5)
    token_rows = tokens.reshape(seqrows * qlength, width)
    queries = (matmul(token_rows, querymap) + querybias.astype(jnp.float32)).astype(jnp.bfloat16)
    keys_local = matmul(token_rows, keymap).astype(jnp.bfloat16)
    values_local = (matmul(token_rows, valuemap) + valuebias.astype(jnp.float32)).astype(
        jnp.bfloat16
    )
    keys_all, values_all = (
        lax.all_gather(keys_local.reshape(seqrows, qlength, width), "seq", axis=1, tiled=True),
        lax.all_gather(values_local.reshape(seqrows, qlength, width), "seq", axis=1, tiled=True),
    )
    query_heads = queries.reshape(seqrows, qlength, H, HD)
    key_heads = keys_all.reshape(seqrows, klength, H, HD)
    value_heads = values_all.reshape(seqrows, klength, H, HD)

    def attend(operands):
        query_one, key_one, value_one, prior_one, same_one = operands
        scores = jnp.einsum("qhe,khe->hqk", query_one, key_one, preferred_element_type=jnp.float32)
        logits = prior_one.astype(jnp.float32) + scores * factor
        masked = jnp.where(same_one, logits, mask_fill)
        row_peak = jnp.max(masked, -1, keepdims=True)
        exponent = jnp.exp(masked - row_peak)
        row_total = jnp.sum(exponent, -1, keepdims=True)
        attention = (exponent / row_total).astype(jnp.bfloat16)
        context = jnp.einsum(
            "hqk,khe->qhe", attention, value_one, preferred_element_type=jnp.float32
        )
        return (
            logits.astype(jnp.bfloat16),
            context.astype(jnp.bfloat16),
            row_peak + jnp.log(row_total),
        )

    raw_logits, context, log_total = lax.map(
        attend, (query_heads, key_heads, value_heads, prev_logits, same_segment)
    )
    context = context.reshape(seqrows * qlength, width)
    attended = matmul(context, mixmap) + mixbias.astype(jnp.float32)
    unit_first, scale_first = normalize(token_rows.astype(jnp.float32) + attended)
    normed = (unit_first * normgain.astype(jnp.float32) + normbias.astype(jnp.float32)).astype(
        jnp.bfloat16
    )
    inner_pre = matmul(normed, expandmap) + expandbias.astype(jnp.float32)
    active = jax.nn.gelu(inner_pre, approximate=False).astype(jnp.bfloat16)
    second = normed.astype(jnp.float32) + (
        matmul(active, shrinkmap) + shrinkbias.astype(jnp.float32)
    )
    unit_second, scale_second = normalize(second)
    layer_out = unit_second * outgain.astype(jnp.float32) + outbias.astype(jnp.float32)
    return (
        weights,
        queries,
        key_heads,
        value_heads,
        log_total,
        context,
        unit_first,
        scale_first,
        normed,
        inner_pre,
        active,
        unit_second,
        scale_second,
        raw_logits,
        layer_out,
    )


def body(
    tokens,
    prev_logits,
    segment_ids,
    out_cotangent,
    logit_cotangent,
    querymap,
    querybias,
    keymap,
    valuemap,
    valuebias,
    mixmap,
    mixbias,
    normgain,
    normbias,
    expandmap,
    expandbias,
    shrinkmap,
    shrinkbias,
    outgain,
    outbias,
):
    shards = (
        querymap,
        querybias,
        keymap,
        valuemap,
        valuebias,
        mixmap,
        mixbias,
        normgain,
        normbias,
        expandmap,
        expandbias,
        shrinkmap,
        shrinkbias,
        outgain,
        outbias,
    )
    seqrows, qlength, width = tokens.shape
    klength = segment_ids.shape[1]
    factor = HD ** (-0.5)
    own_segment = lax.dynamic_slice_in_dim(segment_ids, lax.axis_index("seq") * qlength, qlength, 1)
    same_segment = (own_segment[:, :, None] == segment_ids[:, None, :])[:, None]
    first_pass = forward(shards, tokens, prev_logits, same_segment)
    fenced = lax.optimization_barrier((shards, tokens, prev_logits, same_segment, first_pass[14]))
    state = forward(fenced[0], fenced[1], fenced[2], fenced[3])
    (
        weights,
        queries,
        key_heads,
        value_heads,
        log_total,
        context,
        unit_first,
        scale_first,
        normed,
        inner_pre,
        active,
        unit_second,
        scale_second,
        unused_logits,
        unused_output,
    ) = state
    raw_logits = first_pass[13]
    layer_out = first_pass[14]
    (
        querymap,
        querybias,
        keymap,
        valuemap,
        valuebias,
        mixmap,
        mixbias,
        normgain,
        normbias,
        expandmap,
        expandbias,
        shrinkmap,
        shrinkbias,
        outgain,
        outbias,
    ) = weights
    token_rows = tokens.reshape(seqrows * qlength, width)
    upstream = out_cotangent.reshape(seqrows * qlength, width).astype(jnp.float32)
    outgain_grad = jnp.sum(upstream * unit_second, 0)
    outbias_grad = jnp.sum(upstream, 0)
    second_grad = norm_back(upstream, unit_second, scale_second, outgain.astype(jnp.float32))
    branch_grad = second_grad.astype(jnp.bfloat16)
    shrinkbias_grad = column_sum(branch_grad)
    shrinkmap_grad = rows_product(active, branch_grad)
    active_grad = cols_product(branch_grad, shrinkmap)
    unused_value, gelu_pull = jax.vjp(partial(jax.nn.gelu, approximate=False), inner_pre)
    inner_grad = gelu_pull(active_grad)[0].astype(jnp.bfloat16)
    expandbias_grad = column_sum(inner_grad)
    expandmap_grad = rows_product(normed, inner_grad)
    normed_grad = second_grad + cols_product(inner_grad, expandmap)
    normgain_grad = jnp.sum(normed_grad * unit_first, 0)
    normbias_grad = jnp.sum(normed_grad, 0)
    first_grad = norm_back(normed_grad, unit_first, scale_first, normgain.astype(jnp.float32))
    attended_grad = first_grad.astype(jnp.bfloat16)
    mixbias_grad = column_sum(attended_grad)
    mixmap_grad = rows_product(context, attended_grad)
    context_grad = (
        cols_product(attended_grad, mixmap).astype(jnp.bfloat16).reshape(seqrows, qlength, H, HD)
    )
    query_heads = queries.reshape(seqrows, qlength, H, HD)

    def attend_back(operands):
        (
            query_one,
            key_one,
            value_one,
            prior_one,
            same_one,
            total_one,
            upstream_one,
            cotangent_one,
        ) = operands
        scores = jnp.einsum("qhe,khe->hqk", query_one, key_one, preferred_element_type=jnp.float32)
        logits = prior_one.astype(jnp.float32) + scores * factor
        attention = jnp.exp(jnp.where(same_one, logits, mask_fill) - total_one)
        prob_grad = jnp.einsum(
            "qhe,khe->hqk", upstream_one, value_one, preferred_element_type=jnp.float32
        )
        row_dot = jnp.sum(prob_grad * attention, -1, keepdims=True)
        logit_grad = (cotangent_one.astype(jnp.float32) + attention * (prob_grad - row_dot)).astype(
            jnp.bfloat16
        )
        query_part = (
            jnp.einsum("hqk,khe->qhe", logit_grad, key_one, preferred_element_type=jnp.float32)
            * factor
        )
        key_part = (
            jnp.einsum("hqk,qhe->khe", logit_grad, query_one, preferred_element_type=jnp.float32)
            * factor
        )
        value_part = jnp.einsum(
            "hqk,qhe->khe",
            attention.astype(jnp.bfloat16),
            upstream_one,
            preferred_element_type=jnp.float32,
        )
        return (logit_grad, query_part, key_part, value_part)

    logits_grad, query_grad, key_partial, value_partial = lax.map(
        attend_back,
        (
            query_heads,
            key_heads,
            value_heads,
            prev_logits,
            same_segment,
            log_total,
            context_grad,
            logit_cotangent,
        ),
    )
    key_grad, value_grad = (
        lax.psum_scatter(
            key_partial.reshape(seqrows, klength, width).astype(jnp.bfloat16),
            "seq",
            scatter_dimension=1,
            tiled=True,
        ).astype(jnp.float32),
        lax.psum_scatter(
            value_partial.reshape(seqrows, klength, width).astype(jnp.bfloat16),
            "seq",
            scatter_dimension=1,
            tiled=True,
        ).astype(jnp.float32),
    )
    query_grad = query_grad.reshape(seqrows * qlength, width).astype(jnp.bfloat16)
    key_grad = key_grad.reshape(seqrows * qlength, width).astype(jnp.bfloat16)
    value_grad = value_grad.reshape(seqrows * qlength, width).astype(jnp.bfloat16)
    querymap_grad = rows_product(token_rows, query_grad)
    querybias_grad = column_sum(query_grad)
    keymap_grad = rows_product(token_rows, key_grad)
    valuemap_grad = rows_product(token_rows, value_grad)
    valuebias_grad = column_sum(value_grad)
    tokens_grad = (
        first_grad
        + cols_product(query_grad, querymap)
        + cols_product(key_grad, keymap)
        + cols_product(value_grad, valuemap)
    )
    owned = (
        lax.psum_scatter(querymap_grad, ("dp", "seq"), scatter_dimension=0, tiled=True),
        lax.psum_scatter(querybias_grad, ("dp", "seq"), scatter_dimension=0, tiled=True),
        lax.psum_scatter(keymap_grad, ("dp", "seq"), scatter_dimension=0, tiled=True),
        lax.psum_scatter(valuemap_grad, ("dp", "seq"), scatter_dimension=0, tiled=True),
        lax.psum_scatter(valuebias_grad, ("dp", "seq"), scatter_dimension=0, tiled=True),
        lax.psum_scatter(mixmap_grad, ("dp", "seq"), scatter_dimension=0, tiled=True),
        lax.psum_scatter(mixbias_grad, ("dp", "seq"), scatter_dimension=0, tiled=True),
        lax.psum_scatter(normgain_grad, ("dp", "seq"), scatter_dimension=0, tiled=True),
        lax.psum_scatter(normbias_grad, ("dp", "seq"), scatter_dimension=0, tiled=True),
        lax.psum_scatter(expandmap_grad, ("dp", "seq"), scatter_dimension=0, tiled=True),
        lax.psum_scatter(expandbias_grad, ("dp", "seq"), scatter_dimension=0, tiled=True),
        lax.psum_scatter(shrinkmap_grad, ("dp", "seq"), scatter_dimension=0, tiled=True),
        lax.psum_scatter(shrinkbias_grad, ("dp", "seq"), scatter_dimension=0, tiled=True),
        lax.psum_scatter(outgain_grad, ("dp", "seq"), scatter_dimension=0, tiled=True),
        lax.psum_scatter(outbias_grad, ("dp", "seq"), scatter_dimension=0, tiled=True),
    )
    return (
        layer_out.reshape(seqrows, qlength, width).astype(jnp.bfloat16),
        raw_logits,
        tokens_grad.reshape(seqrows, qlength, width).astype(jnp.bfloat16),
        logits_grad,
    ) + tuple(owned)


def solution(mesh):
    in_specs = (
        P("dp", "seq", None),
        P("dp", None, "seq", None),
        P("dp", None),
        P("dp", "seq", None),
        P("dp", None, "seq", None),
        P(("dp", "seq"), None),
        P(("dp", "seq")),
        P(("dp", "seq"), None),
        P(("dp", "seq"), None),
        P(("dp", "seq")),
        P(("dp", "seq"), None),
        P(("dp", "seq")),
        P(("dp", "seq")),
        P(("dp", "seq")),
        P(("dp", "seq"), None),
        P(("dp", "seq")),
        P(("dp", "seq"), None),
        P(("dp", "seq")),
        P(("dp", "seq")),
        P(("dp", "seq")),
    )
    out_specs = (
        P("dp", "seq", None),
        P("dp", None, "seq", None),
        P("dp", "seq", None),
        P("dp", None, "seq", None),
        P(("dp", "seq"), None),
        P(("dp", "seq")),
        P(("dp", "seq"), None),
        P(("dp", "seq"), None),
        P(("dp", "seq")),
        P(("dp", "seq"), None),
        P(("dp", "seq")),
        P(("dp", "seq")),
        P(("dp", "seq")),
        P(("dp", "seq"), None),
        P(("dp", "seq")),
        P(("dp", "seq"), None),
        P(("dp", "seq")),
        P(("dp", "seq")),
        P(("dp", "seq")),
    )
    return jax.shard_map(body, mesh=mesh, in_specs=in_specs, out_specs=out_specs, check_vma=False)
```

profile of v0, /device:TPU:0, one launch (start us, length us, event | category | flops | bytes accessed | tf_op | source)
XLA Modules:
  0.0 1690.0 jit_solution(7666844894113663365)
XLA Ops:
  17.0 42.5 %all-reduce.28 = (bf16[3072]{0:T(1024)(128)(2,1)S(1)}, bf16[768]{0:T(1024)(128)(2,1)S(1)}, bf16[768]{0:T(1024)(128)(2,1)S(1)}, bf16[768]{0:T(1024)(128)(2,1)S(1)...) all-reduce(bf16[3072]{0:T(1024)(128)(2,1)S(1)} %dynamic-update-slic, ...), channel_id=1, replica_groups=mesh['dp'=16,'seq'=2] {'dp','seq'}, use_global_device_ids=true, to_apply=%add.5 | all-reduce | flops 9216 | bytes 36864
  71.7 51.8 %all-gather.19.cloned.1.call-done = bf16[768,768]{1,0:T(8,128)(2,1)} async-done(((bf16[24,768]{1,0:T(8,128)(2,1)}), bf16[768,768]{1,0:T(8,128)(2,1)}) %all-gather.19.cloned.1.call-update) | async-done | bytes 1179664 | tf_op jit(solution)/shard_map/all_gather | solution.py:72
  130.8 48.5 %all-gather.17.cloned.1.call-done = bf16[768,768]{1,0:T(8,128)(2,1)} async-done(((bf16[24,768]{1,0:T(8,128)(2,1)}), bf16[768,768]{1,0:T(8,128)(2,1)}) %all-gather.17.cloned.1.call-update) | async-done | bytes 1179664 | tf_op jit(solution)/shard_map/all_gather | solution.py:70
  214.1 32.1 %while.40 = (s32[]{:T(128)}, bf16[3,12,256,512]{3,2,1,0:T(8,128)(2,1)}, bf16[3,256,12,64]{1,3,2,0:T(8,128)(2,1)}, bf16[3,12,256,512]{3,2,1,0:T(8,128)(2,1)}, bf1...) while((s32[]{:T(128)}, ...), condition=%wide.region_3.4_spmd, body=%wide.region_0.3_spmd.sunk | while | flops 418578944 | bytes 34237024 | solution.py:138
  248.9 14.2 all-gather.27.cloned.1.call-done
  267.5 61.0 %all-gather.29.cloned.1.call-done = bf16[768,3072]{1,0:T(8,128)(2,1)} async-done(((bf16[24,3072]{1,0:T(8,128)(2,1)}), bf16[768,3072]{1,0:T(8,128)(2,1)}) %all-gather.29.cloned.1.call-update) | async-done | bytes 4718608 | tf_op jit(solution)/shard_map/all_gather | solution.py:79
  328.6 64.9 %all-gather.31.cloned.1.call-done = bf16[3072,768]{1,0:T(8,128)(2,1)} async-done(((bf16[96,768]{1,0:T(8,128)(2,1)}), bf16[3072,768]{1,0:T(8,128)(2,1)}) %all-gather.31.cloned.1.call-update) | async-done | bytes 4718608 | tf_op jit(solution)/shard_map/all_gather | solution.py:81
  393.4 31.3 %fusion.143 = (f32[768]{0:T(1024)S(1)}, f32[768,768]{1,0:T(8,128)S(1)}) fusion(f32[768]{0:T(1024)S(1)} %convert_element_type.242, bf16[3072,768]{1,0:T(8,128)(2,1)} %all-gather.31.cloned.1.call-done, bf16[768,3072]{1,0:T(8,128)(2,1)} %all-gather.29.cloned.1.call-done, f32[3072]{0:T(1024)S(1)} %convert_element_type.240, f32[768,768]{1,0:T(8,128)} %copy-done.20, ...), kind=kOutput, calls=%fused_computation.221 | convolution fusion | flops 7411727360 | bytes 14186496 | tf_op jit(solution)/shard_map/dot_general | solution.py:17
  432.6 39.5 %all-reduce.27 = (bf16[768]{0:T(1024)(128)(2,1)S(1)}, bf16[768]{0:T(1024)(128)(2,1)S(1)}, bf16[768]{0:T(1024)(128)(2,1)S(1)}, bf16[768]{0:T(1024)(128)(2,1)S(1)}...) all-reduce(bf16[768]{0:T(1024)(128)(2,1)S(1)} %dynamic-update-slice, ...), channel_id=1, replica_groups=mesh['dp'=16,'seq'=2] {'dp','seq'}, use_global_device_ids=true, to_apply=%add.10 | all-reduce | flops 8448 | bytes 33792
  483.1 52.2 %all-gather.39.cloned.1.call-done = bf16[768,768]{1,0:T(8,128)(2,1)} async-done(((bf16[24,768]{1,0:T(8,128)(2,1)}), bf16[768,768]{1,0:T(8,128)(2,1)}) %all-gather.39.cloned.1.call-update) | async-done | bytes 1179664 | tf_op jit(solution)/shard_map/all_gather | solution.py:72
  543.0 48.1 %all-gather.37.cloned.1.call-done = bf16[768,768]{1,0:T(8,128)(2,1)} async-done(((bf16[24,768]{1,0:T(8,128)(2,1)}), bf16[768,768]{1,0:T(8,128)(2,1)}) %all-gather.37.cloned.1.call-update) | async-done | bytes 1179664 | tf_op jit(solution)/shard_map/all_gather | solution.py:70
  620.1 31.9 %while.41 = (s32[]{:T(128)}, bf16[3,256,12,64]{1,3,2,0:T(8,128)(2,1)}, f32[3,12,256,1]{2,1,3,0:T(8,128)}, bf16[3,512,12,64]{1,3,2,0:T(8,128)(2,1)}, pred[3,1,256...) while((s32[]{:T(128)}, ...), condition=%wide.region_11.12_spmd, body=%wide.region_8.11_spmd.sunk | while | flops 418575360 | bytes 24878176 | solution.py:138
  655.9 18.1 %all-gather.43.cloned.1.call-done = bf16[768,768]{1,0:T(8,128)(2,1)} async-done(((bf16[24,768]{1,0:T(8,128)(2,1)}), bf16[768,768]{1,0:T(8,128)(2,1)}) %all-gather.43.cloned.1.call-update) | async-done | bytes 1179664 | tf_op jit(solution)/shard_map/all_gather | solution.py:75
  679.2 60.1 %all-gather.45.cloned.1.call-done = bf16[768,3072]{1,0:T(8,128)(2,1)} async-done(((bf16[24,3072]{1,0:T(8,128)(2,1)}), bf16[768,3072]{1,0:T(8,128)(2,1)}) %all-gather.45.cloned.1.call-update) | async-done | bytes 4718608 | tf_op jit(solution)/shard_map/all_gather | solution.py:79
  739.3 28.4 %multiply_convert_fusion = (bf16[768,3072]{1,0:T(8,128)(2,1)}, f32[768,3072]{1,0:T(8,128)}, f32[768,3072]{1,0:T(8,128)}) fusion(f32[3072]{0:T(1024)S(1)} %copy-done.38, bf16[768,3072]{1,0:T(8,128)(2,1)} %all-gather.45.cloned.1.call-done, f32[768,768]{1,0:T(8,128)} %copy-done.6, f32[768]{0:T(1024)S(1)} %convert_element_type.255, ...), kind=kOutput, calls=%fused_computation.89 | convolution fusion | flops 3782541312 | bytes 30695424 | tf_op jit(solution)/shard_map/dot_general | solution.py:17
  767.6 36.4 %all-gather.47.cloned.1.call-done = bf16[3072,768]{1,0:T(8,128)(2,1)} async-done(((bf16[96,768]{1,0:T(8,128)(2,1)}), bf16[3072,768]{1,0:T(8,128)(2,1)}) %all-gather.47.cloned.1.call-update) | async-done | bytes 4718608 | tf_op jit(solution)/shard_map/all_gather | solution.py:81
  855.3 101.8 %while.42 = (s32[]{:T(128)}, bf16[3,12,256,512]{3,2,1,0:T(8,128)(2,1)}, bf16[3,256,12,64]{1,3,2,0:T(8,128)(2,1)}, bf16[3,512,12,64]{1,3,2,0:T(8,128)(2,1)}, bf16...) while((s32[]{:T(128)}, ...), condition=%wide.region_22.23_spmd, body=%wide.region_20.22_spmd.sunk | while | flops 1026100736 | bytes 124696864 | solution.py:318
  1009.9 41.7 %all-reduce.26 = (f32[768]{0:T(1024)S(1)}, f32[768]{0:T(1024)S(1)}, f32[768]{0:T(1024)S(1)}, f32[768]{0:T(1024)S(1)}, f32[768]{0:T(1024)S(1)}, /*index=5*/f32[30...) all-reduce(f32[768]{0:T(1024)S(1)} %reduce_sum.231, ...), channel_id=5, replica_groups=mesh['dp'=16,'seq'=2] {'dp','seq'}, use_global_device_ids=true, to_apply=%region_27.28.clone | all-reduce | flops 9216 | bytes 73728
  1063.6 22.2 %reduce-scatter.19.cloned.1.call-done = f32[24,768]{1,0:T(8,128)} async-done(((f32[768,768]{1,0:T(8,128)}), f32[24,768]{1,0:T(8,128)}) %reduce-scatter.19.cloned.1.call-update) | async-done | bytes 73744 | tf_op jit(solution)/shard_map/reduce_scatter | solution.py:365
  1085.8 104.4 %reduce-scatter.25.cloned.1.call-done = f32[24,768]{1,0:T(8,128)} async-done(((f32[768,768]{1,0:T(8,128)}), f32[24,768]{1,0:T(8,128)}) %reduce-scatter.25.cloned.1.call-update) | async-done | bytes 73744
  1190.2 104.5 %reduce-scatter.27.cloned.1.call-done = f32[24,768]{1,0:T(8,128)} async-done(((f32[768,768]{1,0:T(8,128)}), f32[24,768]{1,0:T(8,128)}) %reduce-scatter.27.cloned.1.call-update) | async-done | bytes 73744
  1294.7 104.5 %reduce-scatter.29.cloned.1.call-done = f32[24,768]{1,0:T(8,128)} async-done(((f32[768,768]{1,0:T(8,128)}), f32[24,768]{1,0:T(8,128)}) %reduce-scatter.29.cloned.1.call-update) | async-done | bytes 73744
  1399.3 142.0 %reduce-scatter.23.cloned.1.call-done = f32[96,768]{1,0:T(8,128)} async-done(((f32[3072,768]{1,0:T(8,128)}), f32[96,768]{1,0:T(8,128)}) %reduce-scatter.23.cloned.1.call-update) | async-done | bytes 294928 | tf_op jit(solution)/shard_map/reduce_scatter | solution.py:371
  1541.2 141.7 %reduce-scatter.21.cloned.1.call-done = f32[24,3072]{1,0:T(8,128)} async-done(((f32[768,3072]{1,0:T(8,128)}), f32[24,3072]{1,0:T(8,128)}) %reduce-scatter.21.cloned.1.call-update) | async-done | bytes 294928 | tf_op jit(solution)/shard_map/reduce_scatter | solution.py:369
  (367 shorter events, 416.4 us)
Async XLA Ops:
  7.2 60.6 %all-gather.23.cloned.1.call-start = ((), (), s32[]{:S(2)}) async-start(), calls=%async_computation.11 | async-start | bytes 1216512 | tf_op jit(solution)/shard_map/all_gather | solution.py:73
  7.9 115.6 %all-gather.19.cloned.1.call-start = ((), (), s32[]{:S(2)}) async-start(), calls=%async_computation.9 | async-start | bytes 1216512 | tf_op jit(solution)/shard_map/all_gather | solution.py:72
  8.7 170.6 %all-gather.17.cloned.1.call-start = ((), (), s32[]{:S(2)}) async-start(), calls=%async_computation.8 | async-start | bytes 1216512 | tf_op jit(solution)/shard_map/all_gather | solution.py:70
  9.4 181.7 %all-gather.25.cloned.1.call-start = ((), (), s32[]{:S(2)}) async-start(), calls=%async_computation.12 | async-start | bytes 3538944 | tf_op jit(solution)/shard_map/all_gather | solution.py:114
  71.7 133.6 %all-gather.21.cloned.1.call-start = ((), (), s32[]{:S(2)}) async-start(), calls=%async_computation.10 | async-start | bytes 3538944 | tf_op jit(solution)/shard_map/all_gather | solution.py:113
  126.9 136.2 %all-gather.27.cloned.1.call-start = ((), (), s32[]{:S(2)}) async-start(), calls=%async_computation.13 | async-start | bytes 1216512 | tf_op jit(solution)/shard_map/all_gather | solution.py:75
  127.5 201.1 %all-gather.29.cloned.1.call-start = ((), (), s32[]{:S(2)}) async-start(), calls=%async_computation.14 | async-start | bytes 4866048 | tf_op jit(solution)/shard_map/all_gather | solution.py:79
  128.2 265.2 %all-gather.31.cloned.1.call-start = ((), (), s32[]{:S(2)}) async-start(), calls=%async_computation.15 | async-start | bytes 4866048 | tf_op jit(solution)/shard_map/all_gather | solution.py:81
  129.0 350.7 %all-gather.33.cloned.1.call-start = ((), (), s32[]{:S(2)}) async-start(), calls=%async_computation.16 | async-start | bytes 1216512 | tf_op jit(solution)/shard_map/all_gather | solution.py:73
  426.9 108.4 %all-gather.39.cloned.1.call-start = ((), (), s32[]{:S(2)}) async-start(), calls=%async_computation.19 | async-start | bytes 1216512 | tf_op jit(solution)/shard_map/all_gather | solution.py:72
  427.5 163.5 %all-gather.37.cloned.1.call-start = ((), (), s32[]{:S(2)}) async-start(), calls=%async_computation.18 | async-start | bytes 1216512 | tf_op jit(solution)/shard_map/all_gather | solution.py:70
  428.3 174.1 %all-gather.35.cloned.1.call-start = ((), (), s32[]{:S(2)}) async-start(), calls=%async_computation.17 | async-start | bytes 3538944 | tf_op jit(solution)/shard_map/all_gather | solution.py:114
  483.1 133.0 %all-gather.41.cloned.1.call-start = ((), (), s32[]{:S(2)}) async-start(), calls=%async_computation.20 | async-start | bytes 3538944 | tf_op jit(solution)/shard_map/all_gather | solution.py:113
  538.7 135.2 %all-gather.43.cloned.1.call-start = ((), (), s32[]{:S(2)}) async-start(), calls=%async_computation.21 | async-start | bytes 1216512 | tf_op jit(solution)/shard_map/all_gather | solution.py:75
  539.3 199.9 %all-gather.45.cloned.1.call-start = ((), (), s32[]{:S(2)}) async-start(), calls=%async_computation.22 | async-start | bytes 4866048 | tf_op jit(solution)/shard_map/all_gather | solution.py:79
  539.9 264.1 %all-gather.47.cloned.1.call-start = ((), (), s32[]{:S(2)}) async-start(), calls=%async_computation.23 | async-start | bytes 4866048 | tf_op jit(solution)/shard_map/all_gather | solution.py:81
  542.9 425.5 %reduce-scatter.15.cloned.1.call-start = ((), (), s32[]{:S(2)}) async-start(), calls=%async_computation.24 | async-start | bytes 3538944 | tf_op jit(solution)/shard_map/reduce_scatter | solution.py:332
  957.1 21.7 %reduce-scatter.17.cloned.1.call-start = ((), (), s32[]{:S(2)}) async-start(), calls=%async_computation.25 | async-start | bytes 3538944 | tf_op jit(solution)/shard_map/reduce_scatter | solution.py:338
  957.7 128.1 %reduce-scatter.19.cloned.1.call-start = ((), (), s32[]{:S(2)}) async-start(), calls=%async_computation.26 | async-start | bytes 2433024 | tf_op jit(solution)/shard_map/reduce_scatter | solution.py:365
  961.6 228.6 %reduce-scatter.25.cloned.1.call-start = ((), (), s32[]{:S(2)}) async-start(), calls=%async_computation.29 | async-start | bytes 2433024
  968.4 326.4 %reduce-scatter.27.cloned.1.call-start = ((), (), s32[]{:S(2)}) async-start(), calls=%async_computation.30 | async-start | bytes 2433024
  973.2 426.1 %reduce-scatter.29.cloned.1.call-start = ((), (), s32[]{:S(2)}) async-start(), calls=%async_computation.31 | async-start | bytes 2433024
  983.6 557.6 %reduce-scatter.23.cloned.1.call-start = ((), (), s32[]{:S(2)}) async-start(), calls=%async_computation.28 | async-start | bytes 9732096 | tf_op jit(solution)/shard_map/reduce_scatter | solution.py:371
  994.2 688.8 %reduce-scatter.21.cloned.1.call-start = ((), (), s32[]{:S(2)}) async-start(), calls=%async_computation.27 | async-start | bytes 9732096 | tf_op jit(solution)/shard_map/reduce_scatter | solution.py:369
  (62 other events, 1012.8 us)
Sparse Core Ops, SparseCore 0:
  10.9 56.8 all-gather.22
  70.7 52.7 all-gather.18
  126.4 52.8 all-gather.16
  181.2 9.8 all-gather.24
  193.1 12.1 all-gather.20
  208.0 55.0 all-gather.26
  266.0 62.4 all-gather.28
  331.5 61.9 all-gather.30
  427.1 52.5 all-gather.32
  482.4 52.8 all-gather.38
  538.2 52.8 all-gather.36
  592.5 9.8 all-gather.34
  603.9 12.1 all-gather.40
  618.8 55.1 all-gather.42
  676.7 62.4 all-gather.44
  742.0 61.9 all-gather.46
  957.2 8.2 reduce-scatter.14
  967.6 11.1 reduce-scatter.16
  984.7 101.0 reduce-scatter.18
  1091.5 98.6 reduce-scatter.24
  1196.1 98.6 reduce-scatter.26
  1300.6 98.6 reduce-scatter.28
  1405.7 135.4 reduce-scatter.22
  1547.5 135.3 reduce-scatter.20
where the time goes:
time: 1700 us; the launch traced here: 1690 us
  waiting for transfers between devices  1130 us (66%)
  matrix products  260 us (15%)
  blocking collectives  124 us (7%)
  local copies, waits for them, and re-layouts  102 us (6%)
  other arithmetic  62.3 us (4%)
    unnamed x27, waiting for transfers between devices  320 us
    reduce_scatter x1, waiting for transfers between devices, body(): lax.psum_scatter(shrinkmap_grad, ('dp', 'seq'), scatter_dimension=0, tile...  142 us
    reduce_scatter x1, waiting for transfers between devices, body(): lax.psum_scatter(expandmap_grad, ('dp', 'seq'), scatter_dimension=0, tile...  142 us
    unnamed x3, blocking collectives  124 us
    all_gather x2, waiting for transfers between devices, forward(): lax.all_gather(expandmap, ('dp', 'seq'), axis=0, tiled=True)  121 us
    all_gather x2, waiting for transfers between devices, forward(): lax.all_gather(keymap, ('dp', 'seq'), axis=0, tiled=True)  104 us
    all_gather x2, waiting for transfers between devices, forward(): lax.all_gather(shrinkmap, ('dp', 'seq'), axis=0, tiled=True)  101 us
    all_gather x2, waiting for transfers between devices, forward(): lax.all_gather(querymap, ('dp', 'seq'), axis=0, tiled=True)  96.6 us
  transfers between devices with their start and end apart: 24, of which 23 were waited for; matrix products, arithmetic and copies ran while one was open for 13% of the time, Pallas kernels for 0%

commit v1 on v0

v1 whole, which is shorter than its diff:
```python
from functools import partial

import jax
import jax.numpy as jnp
from jax import lax
from jax.sharding import PartitionSpec as P

H = 12
HD = 64


norm_eps = 1e-06
mask_fill = -1e30


def matmul(left_side, right_side):
    return jnp.dot(left_side, right_side, preferred_element_type=jnp.float32)


def rows_product(left_side, right_side):
    return lax.dot_general(
        left_side, right_side, (((0,), (0,)), ((), ())), preferred_element_type=jnp.float32
    )


def cols_product(left_side, right_side):
    return lax.dot_general(
        left_side, right_side, (((1,), (1,)), ((), ())), preferred_element_type=jnp.float32
    )


def column_sum(matrix):
    return jnp.sum(matrix.astype(jnp.float32), 0)


def normalize(hidden):
    center = hidden - jnp.mean(hidden, -1, keepdims=True)
    scaled = lax.rsqrt(jnp.mean(center * center, -1, keepdims=True) + norm_eps)
    return (center * scaled, scaled)


def norm_back(upstream, unit_rows, scaled, gain_row):
    pulled = upstream * gain_row
    return scaled * (
        pulled
        - jnp.mean(pulled, -1, keepdims=True)
        - unit_rows * jnp.mean(pulled * unit_rows, -1, keepdims=True)
    )

AXES = ("dp", "seq")
VECTORS = (1, 4, 6, 7, 8, 10, 12, 13, 14)


def gather(block):
    return lax.all_gather(block, AXES, axis=0, tiled=False)


def body(tokens, prev_logits, segment_ids, out_cotangent, logit_cotangent, *shards):
    seqrows, qlength, width = tokens.shape
    klength = segment_ids.shape[1]
    factor = HD ** (-0.5)
    slots = seqrows * qlength
    devices = lax.axis_size(AXES)
    own_segment = lax.dynamic_slice_in_dim(segment_ids, lax.axis_index("seq") * qlength, qlength, 1)
    same_segment = (own_segment[:, :, None] == segment_ids[:, None, :])[:, None]
    (
        querymap, querybias, keymap, valuemap, valuebias, mixmap, mixbias, normgain, normbias,
        expandmap, expandbias, shrinkmap, shrinkbias, outgain, outbias,
    ) = shards
    own = querymap.shape[0]
    hidden = expandmap.shape[1]
    vectors = jnp.concatenate([shards[i] for i in VECTORS])
    vector_size = vectors.shape[0]
    vector_row = jnp.pad(vectors, (0, width - vector_size))[None]
    first_pack = gather(jnp.concatenate([querymap, keymap, valuemap, vector_row]))
    rest_pack = gather(jnp.concatenate([mixmap, shrinkmap, expandmap.reshape(-1, width)]))
    querymap, keymap, valuemap = [
        first_pack[:, i * own : (i + 1) * own].reshape(width, width) for i in range(3)
    ]
    vector_all = first_pack[:, 3 * own, :vector_size].astype(jnp.float32)
    sizes = [shards[i].shape[0] for i in VECTORS]
    parts, at = [], 0
    for size in sizes:
        parts.append(vector_all[:, at : at + size].reshape(-1))
        at += size
    querybias, valuebias, mixbias, normgain, normbias, expandbias, shrinkbias, outgain, outbias = parts
    wide = own * hidden // width
    mixmap = rest_pack[:, :own].reshape(width, width)
    shrinkmap = rest_pack[:, own : own + wide].reshape(hidden, width)
    expandmap = rest_pack[:, own + wide :].reshape(width, hidden)

    token_rows = tokens.reshape(slots, width)
    queries = (matmul(token_rows, querymap) + querybias).astype(jnp.bfloat16)
    keys_local = matmul(token_rows, keymap).astype(jnp.bfloat16)
    values_local = (matmul(token_rows, valuemap) + valuebias).astype(jnp.bfloat16)
    both = lax.all_gather(
        jnp.stack([keys_local, values_local]).reshape(2, seqrows, qlength, width), "seq", axis=2, tiled=True
    )
    query_heads = queries.reshape(seqrows, qlength, H, HD)
    key_heads = both[0].reshape(seqrows, klength, H, HD)
    value_heads = both[1].reshape(seqrows, klength, H, HD)

    def attend(operands):
        query_one, key_one, value_one, prior_one, same_one = operands
        scores = jnp.einsum("qhe,khe->hqk", query_one, key_one, preferred_element_type=jnp.float32)
        logits = prior_one.astype(jnp.float32) + scores * factor
        masked = jnp.where(same_one, logits, mask_fill)
        row_peak = jnp.max(masked, -1, keepdims=True)
        exponent = jnp.exp(masked - row_peak)
        attention = (exponent / jnp.sum(exponent, -1, keepdims=True)).astype(jnp.bfloat16)
        context = jnp.einsum("hqk,khe->qhe", attention, value_one, preferred_element_type=jnp.float32)
        return logits.astype(jnp.bfloat16), context.astype(jnp.bfloat16), attention

    raw_logits, context, attention_all = lax.map(
        attend, (query_heads, key_heads, value_heads, prev_logits, same_segment)
    )
    context = context.reshape(slots, width)
    attended = matmul(context, mixmap) + mixbias
    unit_first, scale_first = normalize(token_rows.astype(jnp.float32) + attended)
    normed = (unit_first * normgain + normbias).astype(jnp.bfloat16)
    inner_pre = matmul(normed, expandmap) + expandbias
    active, gelu_slope = jax.jvp(
        partial(jax.nn.gelu, approximate=False), (inner_pre,), (jnp.ones_like(inner_pre),)
    )
    active = active.astype(jnp.bfloat16)
    gelu_slope = gelu_slope.astype(jnp.bfloat16)
    second = normed.astype(jnp.float32) + (matmul(active, shrinkmap) + shrinkbias)
    unit_second, scale_second = normalize(second)
    layer_out = unit_second * outgain + outbias

    upstream = out_cotangent.reshape(slots, width).astype(jnp.float32)
    outgain_grad = jnp.sum(upstream * unit_second, 0)
    outbias_grad = jnp.sum(upstream, 0)
    second_grad = norm_back(upstream, unit_second, scale_second, outgain)
    branch_grad = second_grad.astype(jnp.bfloat16)
    shrinkbias_grad = column_sum(branch_grad)
    shrinkmap_grad = rows_product(active, branch_grad)
    active_grad = cols_product(branch_grad, shrinkmap)
    inner_grad = (active_grad * gelu_slope.astype(jnp.float32)).astype(jnp.bfloat16)
    expandbias_grad = column_sum(inner_grad)
    expandmap_grad = rows_product(normed, inner_grad)
    early = lax.psum_scatter(
        jnp.concatenate(
            [
                shrinkmap_grad.astype(jnp.bfloat16).reshape(devices, wide, width),
                expandmap_grad.astype(jnp.bfloat16).reshape(devices, wide, width),
            ],
            1,
        ),
        AXES,
        scatter_dimension=0,
        tiled=False,
    ).astype(jnp.float32)
    normed_grad = second_grad + cols_product(inner_grad, expandmap)
    normgain_grad = jnp.sum(normed_grad * unit_first, 0)
    normbias_grad = jnp.sum(normed_grad, 0)
    first_grad = norm_back(normed_grad, unit_first, scale_first, normgain)
    attended_grad = first_grad.astype(jnp.bfloat16)
    mixbias_grad = column_sum(attended_grad)
    mixmap_grad = rows_product(context, attended_grad)
    context_grad = cols_product(attended_grad, mixmap).astype(jnp.bfloat16).reshape(seqrows, qlength, H, HD)

    def attend_back(operands):
        query_one, key_one, value_one, attention_one, upstream_one, cotangent_one = operands
        attention = attention_one.astype(jnp.float32)
        prob_grad = jnp.einsum("qhe,khe->hqk", upstream_one, value_one, preferred_element_type=jnp.float32)
        row_dot = jnp.sum(prob_grad * attention, -1, keepdims=True)
        logit_grad = (cotangent_one.astype(jnp.float32) + attention * (prob_grad - row_dot)).astype(jnp.bfloat16)
        query_part = jnp.einsum("hqk,khe->qhe", logit_grad, key_one, preferred_element_type=jnp.float32) * factor
        key_part = jnp.einsum("hqk,qhe->khe", logit_grad, query_one, preferred_element_type=jnp.float32) * factor
        value_part = jnp.einsum("hqk,qhe->khe", attention_one, upstream_one, preferred_element_type=jnp.float32)
        return logit_grad, query_part.astype(jnp.bfloat16), jnp.stack([key_part, value_part]).astype(jnp.bfloat16)

    logits_grad, query_grad, both_partial = lax.map(
        attend_back, (query_heads, key_heads, value_heads, attention_all, context_grad, logit_cotangent)
    )
    both_grad = lax.psum_scatter(
        both_partial.reshape(seqrows, 2, klength, width), "seq", scatter_dimension=2, tiled=True
    )
    query_grad = query_grad.reshape(slots, width)
    key_grad = both_grad[:, 0].reshape(slots, width)
    value_grad = both_grad[:, 1].reshape(slots, width)
    querymap_grad = rows_product(token_rows, query_grad)
    querybias_grad = column_sum(query_grad)
    keymap_grad = rows_product(token_rows, key_grad)
    valuemap_grad = rows_product(token_rows, value_grad)
    valuebias_grad = column_sum(value_grad)
    tokens_grad = (
        first_grad
        + cols_product(query_grad, querymap)
        + cols_product(key_grad, keymap)
        + cols_product(value_grad, valuemap)
    )
    vector_grads = jnp.concatenate(
        [
            grad.reshape(devices, -1)
            for grad in (
                querybias_grad, valuebias_grad, mixbias_grad, normgain_grad, normbias_grad,
                expandbias_grad, shrinkbias_grad, outgain_grad, outbias_grad,
            )
        ],
        1,
    )
    vector_grads = jnp.pad(vector_grads, ((0, 0), (0, width - vector_size)))[:, None]
    late = lax.psum_scatter(
        jnp.concatenate(
            [
                querymap_grad.reshape(devices, own, width),
                keymap_grad.reshape(devices, own, width),
                valuemap_grad.reshape(devices, own, width),
                mixmap_grad.reshape(devices, own, width),
                vector_grads,
            ],
            1,
        ).astype(jnp.bfloat16),
        AXES,
        scatter_dimension=0,
        tiled=False,
    ).astype(jnp.float32)
    vector_own, parts, at = late[4 * own], [], 0
    for size in sizes:
        parts.append(vector_own[at : at + size])
        at += size
    (
        querybias_grad, valuebias_grad, mixbias_grad, normgain_grad, normbias_grad,
        expandbias_grad, shrinkbias_grad, outgain_grad, outbias_grad,
    ) = parts
    owned = (
        late[:own], querybias_grad, late[own : 2 * own], late[2 * own : 3 * own], valuebias_grad,
        late[3 * own : 4 * own], mixbias_grad, normgain_grad, normbias_grad,
        early[wide:].reshape(own, hidden), expandbias_grad, early[:wide], shrinkbias_grad,
        outgain_grad, outbias_grad,
    )
    return (
        layer_out.reshape(seqrows, qlength, width).astype(jnp.bfloat16),
        raw_logits,
        tokens_grad.reshape(seqrows, qlength, width).astype(jnp.bfloat16),
        logits_grad,
    ) + owned


def solution(mesh):
    in_specs = (
        P("dp", "seq", None),
        P("dp", None, "seq", None),
        P("dp", None),
        P("dp", "seq", None),
        P("dp", None, "seq", None),
        P(("dp", "seq"), None),
        P(("dp", "seq")),
        P(("dp", "seq"), None),
        P(("dp", "seq"), None),
        P(("dp", "seq")),
        P(("dp", "seq"), None),
        P(("dp", "seq")),
        P(("dp", "seq")),
        P(("dp", "seq")),
        P(("dp", "seq"), None),
        P(("dp", "seq")),
        P(("dp", "seq"), None),
        P(("dp", "seq")),
        P(("dp", "seq")),
        P(("dp", "seq")),
    )
    out_specs = (
        P("dp", "seq", None),
        P("dp", None, "seq", None),
        P("dp", "seq", None),
        P("dp", None, "seq", None),
        P(("dp", "seq"), None),
        P(("dp", "seq")),
        P(("dp", "seq"), None),
        P(("dp", "seq"), None),
        P(("dp", "seq")),
        P(("dp", "seq"), None),
        P(("dp", "seq")),
        P(("dp", "seq")),
        P(("dp", "seq")),
        P(("dp", "seq"), None),
        P(("dp", "seq")),
        P(("dp", "seq"), None),
        P(("dp", "seq")),
        P(("dp", "seq")),
        P(("dp", "seq")),
    )
    return jax.shard_map(body, mesh=mesh, in_specs=in_specs, out_specs=out_specs, check_vma=False)
```

time: 1700 us -> 638 us (0.38)
  waiting for transfers between devices: 1130 us -> 297 us
  blocking collectives: 124 us -> 0 us
  matrix products: 260 us -> 137 us
  local copies, waits for them, and re-layouts: 102 us -> 123 us
    all_gather x16 -> x3, waiting for transfers between devices: 493 us -> 86.9 us  [the longest x2 86.9 us: gather(): return lax.all_gather(block, AXES, axis=0, tiled=False)]
    unnamed x27 -> x6, waiting for transfers between devices: 320 us -> 0.1 us
    unnamed x3 -> x0, blocking collectives: 124 us -> none
    reduce_scatter x5 -> x3, waiting for transfers between devices: 312 us -> 210 us  [the longest x1 110 us: body(): lax.psum_scatter(jnp.concatenate([querymap_grad.reshape(devices, own, wid...]
    dot_general x11 -> x6, matrix products: 93.1 us -> 40.6 us  [matmul(): return jnp.dot(left_side, right_side, preferred_element_type=jnp.float32)]
    slice x0 -> x15, local copies, waits for them, and re-layouts: none -> 31.6 us  [the longest x2 9.19 us: body(): value_heads = both[1].reshape(seqrows, klength, H, HD)]
    dot_general x6 -> x3, matrix products: 28.5 us -> 8.06 us  [attend_back(): jnp.einsum('hqk,qhe->khe', attention_one, upstream_one, preferred_element...]
    unnamed x143 -> x118, local copies, waits for them, and re-layouts: 37.7 us -> 18.2 us
  transfers between devices with their start and end apart: 24 -> 6, of which waited for: 23 -> 4; matrix products, arithmetic and copies ran while one was open for 13% -> 23% of each run, Pallas kernels for 0% -> 0%
where the time goes in v1:
time: 638 us; the launch traced here: 633 us
  waiting for transfers between devices  297 us (47%)
  matrix products  137 us (21%)
  local copies, waits for them, and re-layouts  123 us (19%)
  other arithmetic  60 us (9%)
  between operations  15 us (2%)
    reduce_scatter x1, waiting for transfers between devices, body(): lax.psum_scatter(jnp.concatenate([querymap_grad.reshape(devices, own, wid...  110 us
    reduce_scatter x1, waiting for transfers between devices, body(): lax.psum_scatter(jnp.concatenate([shrinkmap_grad.astype(jnp.bfloat16).res...  99.8 us
    all_gather x2, waiting for transfers between devices, gather(): return lax.all_gather(block, AXES, axis=0, tiled=False)  86.9 us
    dot_general x6, matrix products, matmul(): return jnp.dot(left_side, right_side, preferred_element_type=jnp.float32)  40.6 us
    dot_general x6, matrix products, cols_product(): lax.dot_general(left_side, right_side, (((1,), (1,)), ((), ())), preferre...  29.2 us
    dot_general x6, matrix products, rows_product(): lax.dot_general(left_side, right_side, (((0,), (0,)), ((), ())), preferre...  22.5 us
    sub x3, other arithmetic, attend_back(): prob_grad - row_dot  21.4 us
    unnamed x118, local copies, waits for them, and re-layouts  18.2 us
  transfers between devices with their start and end apart: 6, of which 4 were waited for; matrix products, arithmetic and copies ran while one was open for 23% of the time, Pallas kernels for 0%

profile of v1, /device:TPU:0, one launch (start us, length us, event | category | flops | bytes accessed | tf_op | source)
XLA Modules:
  0.0 632.6 jit_solution(15294128923085166255)
XLA Ops:
  7.2 6.1 concatenate.29
  14.9 63.7 %all-gather.11.cloned.1.call-done = bf16[32,73,768]{2,1,0:T(8,128)(2,1)} async-done(((bf16[1,73,768]{2,1,0:T(8,128)(2,1)}), bf16[32,73,768]{2,1,0:T(8,128)(2,1)}) %all-gather.11.cloned.1.call-update) | async-done | bytes 3588112 | tf_op jit(solution)/shard_map/all_gather | solution.py:55
  102.4 4.9 fusion.76
  114.4 4.8 broadcast.123.clone
  119.2 4.6 broadcast.123.clone.1
  125.0 39.2 %while.28 = (s32[]{:T(128)}, bf16[3,12,256,512]{3,2,1,0:T(8,128)(2,1)}, bf16[3,256,12,64]{1,3,2,0:T(8,128)(2,1)}, bf16[3,12,256,512]{3,2,1,0:T(8,128)(2,1)}, bf1...) while((s32[]{:T(128)}, ...), condition=%wide.region_3.4_spmd, body=%wide.region_0.3_spmd.sunk | while | flops 418578944 | bytes 43674728 | solution.py:114
  167.8 23.2 %all-gather.9.cloned.1.call-done = bf16[6912,768]{1,0:T(8,128)(2,1)} async-done(((bf16[216,768]{1,0:T(8,128)(2,1)}), bf16[6912,768]{1,0:T(8,128)(2,1)}) %all-gather.9.cloned.1.call-update) | async-done | bytes 10616848 | tf_op jit(solution)/shard_map/all_gather | solution.py:55
  192.4 8.6 %fusion.75 = (bf16[32,96,768]{2,1,0:T(8,128)(2,1)}, bf16[32,96,768]{2,1,0:T(8,128)(2,1)}) fusion(bf16[32,216,768]{2,1,0:T(8,128)(2,1)} %bitcast.257), kind=kLoop, calls=%fused_computation.159 | loop fusion | bytes 18874368 | tf_op jit(solution)/shard_map/slice | solution.py:89
  204.2 8.5 %reshape.284 = bf16[768,3072]{1,0:T(8,128)(2,1)} reshape(bf16[32,96,768]{2,1,0:T(8,128)(2,1)} %get-tuple-element.263) | data formatting | bytes 9437184 | tf_op jit(solution)/shard_map/reshape | solution.py:90
  212.7 28.1 %multiply_convert_fusion.2 = (bf16[768,3072]{1,0:T(8,128)(2,1)S(1)}, f32[768,3072]{1,0:T(8,128)}, f32[768,3072]{1,0:T(8,128)}) fusion(f32[3072]{0:T(1024)} %add.146, bf16[768,3072]{1,0:T(8,128)(2,1)} %reshape.284, f32[768,768]{1,0:T(8,128)} %copy-done.5, f32[768]{0:T(1024)S(1)} %copy-done.44, f32[768]{0:T(1024)S(1)} %copy-done.36, ...), kind=kOutput, calls=%fused_computation.65 | convolution fusion | flops 3782541312 | bytes 30695424 | tf_op jit(solution)/shard_map/dot_general | solution.py:17
  243.0 6.4 %fusion.80 = (f32[768]{0:T(1024)S(1)}, f32[768,768]{1,0:T(8,128)S(1)}) fusion(f32[768]{0:T(1024)S(1)} %copy-done.45, bf16[768,3072]{1,0:T(8,128)(2,1)S(1)} %get-tuple-element.254, bf16[3072,768]{1,0:T(8,128)(2,1)} %bitcast.267, f32[768]{0:T(1024)S(1)} %copy-done.44, f32[768]{0:T(1024)S(1)} %copy-done.36, f32[768]{0:T(1024)S(1)} %add_rsqrt_fusion.1, ...), kind=kOutput, calls=%fused_computation.164 | convolution fusion | flops 3629186304 | bytes 14174208 | tf_op jit(solution)/shard_map/dot_general | solution.py:17
  254.8 13.5 %fusion.81 = (bf16[3072]{0:T(1024)(128)(2,1)}, bf16[768,3072]{1,0:T(8,128)(2,1)}) fusion(f32[768,3072]{1,0:T(8,128)} %get-tuple-element.297, f32[3072]{0:T(1024)S(1)} %copy-done.39, f32[768,3072]{1,0:T(8,128)} %get-tuple-element.255, bf16[3072,768]{1,0:T(8,128)(2,1)} %bitcast.268, f32[768,768]{1,0:T(8,128)S(1)} %get-tuple-element.251), kind=kOutput, calls=%fused_computation.165 | convolution fusion | flops 3659854848 | bytes 30689280 | tf_op jit(solution)/shard_map/dot_general | solution.py:27
  268.4 7.1 %multiply_reduce_fusion = (bf16[768]{0:T(1024)(128)(2,1)}, f32[768]{0:T(1024)S(1)}, f32[768]{0:T(1024)S(1)}, bf16[768]{0:T(1024)(128)(2,1)}, f32[768,768]{1,0:T(8,128)S(1)}) fusion(f32[768,768]{1,0:T(8,128)S(1)} %copy-done.6, f32[768]{0:T(1024)S(1)} %add_rsqrt_fusion.1, f32[768]{0:T(1024)S(1)} %broadcast_multiply_fusion.5, f32[768]{0:T(1024)S(1)} %copy-done.36, ...), kind=kOutput, calls=%fused_computation.92 | convolution fusion | flops 3629773824 | bytes 16533504 | tf_op jit(solution)/shard_map/dot_general | solution.py:27
  280.5 4.7 reshape.314
  289.7 4.8 broadcast.123
  295.7 47.8 %while.29 = (s32[]{:T(128)}, bf16[3,12,256,512]{3,2,1,0:T(8,128)(2,1)}, bf16[3,256,12,64]{1,3,2,0:T(8,128)(2,1)}, bf16[3,2,512,12,64]{2,4,3,1,0:T(8,128)(2,1)}, ...) while((s32[]{:T(128)}, ...), condition=%wide.region_14.15_spmd, body=%wide.region_12.14_spmd.sunk | while | flops 822611456 | bytes 51909232 | solution.py:174
  298.0 7.2 %bitcast_dynamic-update-slice_fusion.8 = (bf16[3,12,256,512]{3,2,1,0:T(8,128)(2,1)}, bf16[12,256,512]{2,1,0:T(8,128)(2,1)S(1)}) fusion(bf16[3,12,256,512]{3,2,1,0:T(8,128)(2,1)} %get-tuple-element.479, s32[]{:T(128)} %get-tuple-element.478, f32[12,256,512]{2,1,0:T(8,128)S(1)} %fusion.145, bf16[3,12,256,512]{3,2,1,0:T(8,128)(2,1)} %get-tuple-element.494, ...), kind=kOutput, calls=%fused_computation.29.clone.1 | output fusion | flops 12586495 | bytes 28312576 | tf_op jit(solution)/shard_map/while/body/eval_jaxpr/sub | solution.py:168
  314.0 7.1 %bitcast_dynamic-update-slice_fusion.8 = (bf16[3,12,256,512]{3,2,1,0:T(8,128)(2,1)}, bf16[12,256,512]{2,1,0:T(8,128)(2,1)S(1)}) fusion(bf16[3,12,256,512]{3,2,1,0:T(8,128)(2,1)} %get-tuple-element.479, s32[]{:T(128)} %get-tuple-element.478, f32[12,256,512]{2,1,0:T(8,128)S(1)} %fusion.145, bf16[3,12,256,512]{3,2,1,0:T(8,128)(2,1)} %get-tuple-element.494, ...), kind=kOutput, calls=%fused_computation.29.clone.1 | output fusion | flops 12586495 | bytes 28312576 | tf_op jit(solution)/shard_map/while/body/eval_jaxpr/sub | solution.py:168
  329.8 7.1 %bitcast_dynamic-update-slice_fusion.8 = (bf16[3,12,256,512]{3,2,1,0:T(8,128)(2,1)}, bf16[12,256,512]{2,1,0:T(8,128)(2,1)S(1)}) fusion(bf16[3,12,256,512]{3,2,1,0:T(8,128)(2,1)} %get-tuple-element.479, s32[]{:T(128)} %get-tuple-element.478, f32[12,256,512]{2,1,0:T(8,128)S(1)} %fusion.145, bf16[3,12,256,512]{3,2,1,0:T(8,128)(2,1)} %get-tuple-element.494, ...), kind=kOutput, calls=%fused_computation.29.clone.1 | output fusion | flops 12586495 | bytes 28312576 | tf_op jit(solution)/shard_map/while/body/eval_jaxpr/sub | solution.py:168
  345.1 8.7 %convolution_convert_fusion.1 = bf16[768,3072]{1,0:T(8,128)(2,1)} fusion(bf16[768,3072]{1,0:T(8,128)(2,1)} %get-tuple-element.302, f32[768,768]{1,0:T(8,128)S(1)} %copy-done.7, f32[768]{0:T(1024)S(1)} %copy-done.44, f32[768]{0:T(1024)S(1)} %copy-done.36, f32[768]{0:T(1024)S(1)} %add_rsqrt_fusion.1, f32[768]{0:T(1024)S(1)} %broadcast_multiply_fusion.5), kind=kOutput, calls=%fused_computation.79 | convolution fusion | flops 3629187072 | bytes 11808768 | tf_op jit(solution)/shard_map/dot_general | solution.py:21
  353.8 8.7 %reshape.302 = bf16[32,96,768]{2,1,0:T(8,128)(2,1)} reshape(bf16[768,3072]{1,0:T(8,128)(2,1)} %convolution_convert_fusion.1) | data formatting | bytes 9437184 | tf_op jit(solution)/shard_map/reshape | solution.py:146
  362.5 6.9 %convolution_convert_fusion.2 = bf16[3072,768]{1,0:T(8,128)(2,1)S(1)} fusion(bf16[768,3072]{1,0:T(8,128)(2,1)} %copy-done.53, f32[768,768]{1,0:T(8,128)S(1)} %copy-done.13), kind=kOutput, calls=%fused_computation.80 | convolution fusion | flops 3626827776 | bytes 11796480 | tf_op jit(solution)/shard_map/dot_general | solution.py:21
  409.0 99.8 %reduce-scatter.8.cloned.1.call-done = bf16[1,192,768]{2,1,0:T(8,128)(2,1)} async-done(((bf16[32,192,768]{2,1,0:T(8,128)(2,1)}), bf16[1,192,768]{2,1,0:T(8,128)(2,1)}) %reduce-scatter.8.cloned.1.call-update) | async-done | bytes 294928 | tf_op jit(solution)/shard_map/reduce_scatter | solution.py:142
  512.3 110.4 %reduce-scatter.6.cloned.1.call-done = bf16[1,97,768]{2,1,0:T(8,128)(2,1)} async-done(((bf16[32,97,768]{2,1,0:T(8,128)(2,1)}), bf16[1,97,768]{2,1,0:T(8,128)(2,1)}) %reduce-scatter.6.cloned.1.call-update) | async-done | bytes 149008 | tf_op jit(solution)/shard_map/reduce_scatter | solution.py:205
  (247 shorter events, 172.7 us)
Async XLA Ops:
  7.2 71.4 %all-gather.11.cloned.1.call-start = ((), (), s32[]{:S(2)}) async-start(), calls=%async_computation.8 | async-start | bytes 4055040 | tf_op jit(solution)/shard_map/all_gather | solution.py:55
  14.8 87.5 %all-gather.7.cloned.1.call-start = ((), (), s32[]{:S(2)}) async-start(), calls=%async_computation.3 | async-start | bytes 7077888 | tf_op jit(solution)/shard_map/all_gather | solution.py:96
  82.7 7.8 %copy-start.16 = (bf16[32,24,768]{2,1,0:T(8,128)(2,1)}, bf16[32,24,768]{2,1,0:T(8,128)(2,1)S(1)}, u32[]{:S(2)}) copy-start(bf16[32,24,768]{2,1,0:T(8,128)(2,1)S(1)} %get-tuple-element.267) | copy-start | bytes 3538948
  86.8 104.2 %all-gather.9.cloned.1.call-start = ((), (), s32[]{:S(2)}) async-start(), calls=%async_computation.7 | async-start | bytes 10948608 | tf_op jit(solution)/shard_map/all_gather | solution.py:55
  88.6 297.2 %reduce-scatter.4.cloned.1.call-start = ((), (), s32[]{:S(2)}) async-start(), calls=%async_computation.4 | async-start | bytes 7077888 | tf_op jit(solution)/shard_map/reduce_scatter | solution.py:177
  93.0 8.4 %copy-start = (bf16[3,256,768]{2,1,0:T(8,128)(2,1)S(1)}, bf16[3,256,768]{2,1,0:T(8,128)(2,1)}, u32[]{:S(2)}) copy-start(bf16[3,256,768]{2,1,0:T(8,128)(2,1)} %param.27) | copy-start | bytes 3538948
  100.8 6.5 %copy-start.26 = (f32[768]{0:T(1024)}, f32[768]{0:T(1024)S(1)}, u32[]{:S(2)}) copy-start(f32[768]{0:T(1024)S(1)} %mul.164) | copy-start | bytes 9220
  192.4 8.6 %copy-start.17 = (bf16[32,24,768]{2,1,0:T(8,128)(2,1)}, bf16[32,24,768]{2,1,0:T(8,128)(2,1)S(1)}, u32[]{:S(2)}) copy-start(bf16[32,24,768]{2,1,0:T(8,128)(2,1)S(1)} %slice.215) | copy-start | bytes 3538948
  192.4 8.6 %copy-start.21 = (bf16[96,8,3,256]{3,1,2,0:T(8,128)(2,1)S(1)}, bf16[96,8,3,256]{3,1,2,0:T(8,128)(2,1)}, u32[]{:S(2)}) copy-start(bf16[96,8,3,256]{3,1,2,0:T(8,128)(2,1)} %copy.79) | copy-start | bytes 3538948
  192.4 8.6 %copy-start.46 = (f32[768]{0:T(1024)S(1)}, f32[768]{0:T(1024)}, u32[]{:S(2)}) copy-start(f32[768]{0:T(1024)} %add.138) | copy-start | bytes 9220
  192.4 8.6 %copy-start.50 = (bf16[3,256,768]{2,1,0:T(8,128)(2,1)S(1)}, bf16[3,256,768]{2,1,0:T(8,128)(2,1)}, u32[]{:S(2)}) copy-start(bf16[3,256,768]{2,1,0:T(8,128)(2,1)} %param.24) | copy-start | bytes 3538948
  204.2 8.5 %copy-start.36 = (f32[768]{0:T(1024)S(1)}, f32[768]{0:T(1024)}, u32[]{:S(2)}) copy-start(f32[768]{0:T(1024)} %mul.154) | copy-start | bytes 9220
  204.2 8.5 %copy-start.44 = (f32[768]{0:T(1024)S(1)}, f32[768]{0:T(1024)}, u32[]{:S(2)}) copy-start(f32[768]{0:T(1024)} %add.143) | copy-start | bytes 9220
  212.7 30.3 %copy-start.6 = (f32[768,768]{1,0:T(8,128)S(1)}, f32[768,768]{1,0:T(8,128)}, u32[]{:S(2)}) copy-start(f32[768,768]{1,0:T(8,128)} %copy-done.5) | copy-start | bytes 7077892
  212.7 30.3 %copy-start.45 = (f32[768]{0:T(1024)S(1)}, f32[768]{0:T(1024)}, u32[]{:S(2)}) copy-start(f32[768]{0:T(1024)} %add.149) | copy-start | bytes 9220
  253.5 14.9 %slice-start = ((s8[4718592]{0:T(1024)(128)(4,1)}), s8[4194304]{0:T(1024)(128)(4,1)S(1)}, s32[]{:S(2)}) async-start(s8[4718592]{0:T(1024)(128)(4,1)} %bitcast.261), calls=%async_computation.9 | async-start | bytes 8388608
  254.8 13.5 %copy-start.12 = (f32[768,768]{1,0:T(8,128)}, f32[768,768]{1,0:T(8,128)S(1)}, u32[]{:S(2)}) copy-start(f32[768,768]{1,0:T(8,128)S(1)} %get-tuple-element.251) | copy-start | bytes 7077892
  254.8 13.5 %slice-start.1 = ((s8[4718592]{0:T(1024)(128)(4,1)}), s8[524288]{0:T(1024)(128)(4,1)S(1)}, s32[]{:S(2)}) async-start(s8[4718592]{0:T(1024)(128)(4,1)} %bitcast.261), calls=%async_computation.10 | async-start | bytes 1048576
  343.5 165.3 %reduce-scatter.8.cloned.1.call-start = ((), (), s32[]{:S(2)}) async-start(), calls=%async_computation.6 | async-start | bytes 9732096 | tf_op jit(solution)/shard_map/reduce_scatter | solution.py:142
  353.8 8.7 %copy-start.13 = (f32[768,768]{1,0:T(8,128)S(1)}, f32[768,768]{1,0:T(8,128)}, u32[]{:S(2)}) copy-start(f32[768,768]{1,0:T(8,128)} %copy-done.12) | copy-start | bytes 7077892
  362.5 6.9 %copy-start.3 = (bf16[32,96,768]{2,1,0:T(8,128)(2,1)S(1)}, bf16[32,96,768]{2,1,0:T(8,128)(2,1)}, u32[]{:S(2)}) copy-start(bf16[32,96,768]{2,1,0:T(8,128)(2,1)} %reshape.302) | copy-start | bytes 14155780
  373.4 6.8 %copy-start.41 = (bf16[768]{0:T(1024)(128)(2,1)S(1)}, bf16[768]{0:T(1024)(128)(2,1)}, u32[]{:S(2)}) copy-start(bf16[768]{0:T(1024)(128)(2,1)} %get-tuple-element.250) | copy-start | bytes 4612
  373.4 7.5 %copy-start.40 = (bf16[768]{0:T(1024)(128)(2,1)S(1)}, bf16[768]{0:T(1024)(128)(2,1)}, u32[]{:S(2)}) copy-start(bf16[768]{0:T(1024)(128)(2,1)} %get-tuple-element.206) | copy-start | bytes 4612
  373.5 249.2 %reduce-scatter.6.cloned.1.call-start = ((), (), s32[]{:S(2)}) async-start(), calls=%async_computation.5 | async-start | bytes 5271552 | tf_op jit(solution)/shard_map/reduce_scatter | solution.py:205
  (38 other events, 94.9 us)
Sparse Core Ops, SparseCore 0:
  15.0 63.5 all-gather.10
  86.9 13.2 all-gather.6
  103.2 87.7 all-gather.8
  343.6 10.9 reduce-scatter.3
  373.5 135.2 reduce-scatter.7
  514.2 108.3 reduce-scatter.5

commit v2 on v1

v2 whole, which is shorter than its diff:
```python
from functools import partial

import jax
import jax.numpy as jnp
from jax import lax
from jax.experimental import pallas as pl
from jax.experimental.pallas import tpu as pltpu
from jax.sharding import PartitionSpec as P

H = 12
HD = 64
PAIR = 2 * HD
MESH = pl.DeviceIdType.MESH
ANY = pl.BlockSpec(memory_space=pl.ANY)
VMEM = pl.BlockSpec(memory_space=pltpu.VMEM)


norm_eps = 1e-06
mask_fill = -1e30


def matmul(left_side, right_side):
    return jnp.dot(left_side, right_side, preferred_element_type=jnp.float32)


def rows_product(left_side, right_side):
    return lax.dot_general(
        left_side, right_side, (((0,), (0,)), ((), ())), preferred_element_type=jnp.float32
    )


def cols_product(left_side, right_side):
    return lax.dot_general(
        left_side, right_side, (((1,), (1,)), ((), ())), preferred_element_type=jnp.float32
    )


def column_sum(matrix):
    return jnp.sum(matrix.astype(jnp.float32), 0)


def normalize(hidden):
    center = hidden - jnp.mean(hidden, -1, keepdims=True)
    scaled = lax.rsqrt(jnp.mean(center * center, -1, keepdims=True) + norm_eps)
    return (center * scaled, scaled)


def norm_back(upstream, unit_rows, scaled, gain_row):
    pulled = upstream * gain_row
    return scaled * (
        pulled
        - jnp.mean(pulled, -1, keepdims=True)
        - unit_rows * jnp.mean(pulled * unit_rows, -1, keepdims=True)
    )


def flip(index, bit):
    return index + bit * (1 - 2 * lax.rem(index // bit, 2))


def flip_mask(index, mask):
    bit = 1
    while bit <= mask:
        if mask & bit:
            index = flip(index, bit)
        bit *= 2
    return index


def masks_of(order):
    masks = [0]
    for place in order:
        masks = masks + [mask ^ (1 << place) for mask in masks]
    return masks


def orders_of(bits):
    first = list(range(bits - 1, -1, -1))
    second = list(first)
    if bits >= 2:
        second[-1], second[-2] = second[-2], second[-1]
    return first, second


def barrier(bits, me, core):
    gate = pltpu.get_barrier_semaphore()
    for place in range(bits):
        pl.semaphore_signal(gate, inc=1, device_id=(flip(me, 1 << place), core), device_id_type=MESH)
    pl.semaphore_signal(gate, inc=1, device_id=(me, 1 - core), device_id_type=MESH)
    pl.semaphore_wait(gate, bits + 1)


def wait_bytes(region, semaphore):
    pltpu.make_async_copy(region, region, semaphore).wait()


class Gather:
    def __init__(self, bits, shards, fulls, hop_sems, core_sems, send_sems, own_sems):
        self.bits, self.shards, self.fulls = bits, shards, fulls
        self.hop_sems, self.core_sems = hop_sems, core_sems
        self.send_sems, self.own_sems = send_sems, own_sems
        self.orders = [orders_of(bits)[i % 2] for i in range(len(shards))]
        self.me, self.core = lax.axis_index("dp"), lax.axis_index("seq")

    def slot(self, mask):
        return flip_mask(self.me, mask) * 2 + self.core

    def own(self, i):
        return pltpu.make_async_copy(self.shards[i], self.fulls[i].at[self.slot(0)], self.own_sems.at[i])

    def send(self, i, mask, device, semaphore):
        slot = self.slot(mask)
        source = self.fulls[i].at[slot] if mask else self.shards[i]
        pltpu.make_async_remote_copy(
            src_ref=source, dst_ref=self.fulls[i].at[slot], send_sem=self.send_sems.at[i],
            recv_sem=semaphore, device_id=device, device_id_type=MESH,
        ).start()

    def phase(self, step):
        for i in range(len(self.shards)):
            masks = masks_of(self.orders[i])
            fresh = masks[:1] if step == 0 else masks[1 << (step - 1) : 1 << step]
            if step == 0:
                self.own(i).start()
            else:
                wait_bytes(self.fulls[i].at[pl.ds(0, len(fresh))], self.hop_sems.at[i, step - 1])
            if step < self.bits:
                partner = (flip(self.me, 1 << self.orders[i][step]), self.core)
                for mask in masks[: 1 << step]:
                    self.send(i, mask, partner, self.hop_sems.at[i, step])
            for mask in fresh:
                self.send(i, mask, (self.me, 1 - self.core), self.core_sems.at[i])

    def finish(self):
        size = 1 << self.bits
        for i in range(len(self.shards)):
            wait_bytes(self.fulls[i].at[pl.ds(0, size)], self.core_sems.at[i])
            wait_bytes(self.fulls[i].at[pl.ds(0, 2 * size - 1)], self.send_sems.at[i])
            self.own(i).wait()

    def phases(self):
        return [partial(self.phase, step) for step in range(self.bits + 1)] + [self.finish]


def gather_scratch(count, bits):
    return [
        pltpu.SemaphoreType.DMA((count, bits)),
        pltpu.SemaphoreType.DMA((count,)),
        pltpu.SemaphoreType.DMA((count,)),
        pltpu.SemaphoreType.DMA((count,)),
    ]


def gather_kernel(bits, count, tokens_ref, *refs):
    shards, (both_ref, *fulls) = refs[:count], refs[count : 2 * count + 1]
    sems = refs[2 * count + 1 : 2 * count + 5]
    token_sems = refs[2 * count + 5]
    me, core = lax.axis_index("dp"), lax.axis_index("seq")
    barrier(bits, me, core)
    gather = Gather(bits, shards, fulls, *sems)
    phases = gather.phases()
    phases[0]()
    mine = pltpu.make_async_copy(tokens_ref, both_ref.at[0], token_sems.at[0])
    other = pltpu.make_async_remote_copy(
        src_ref=tokens_ref, dst_ref=both_ref.at[1], send_sem=token_sems.at[1], recv_sem=token_sems.at[2],
        device_id=(me, 1 - core), device_id_type=MESH,
    )
    mine.start()
    other.start()
    for phase in phases[1:]:
        phase()
    mine.wait()
    other.wait()


def gather_all(bits, tokens, shards):
    count, devices = len(shards), 2 << bits
    outs = [jax.ShapeDtypeStruct((2,) + tokens.shape, tokens.dtype)]
    outs += [jax.ShapeDtypeStruct((devices,) + shard.shape, shard.dtype) for shard in shards]
    return pl.pallas_call(
        partial(gather_kernel, bits, count),
        out_shape=outs,
        in_specs=[VMEM] * (count + 1),
        out_specs=[ANY] * (count + 1),
        scratch_shapes=gather_scratch(count, bits) + [pltpu.SemaphoreType.DMA((3,))],
        compiler_params=pltpu.CompilerParams(collective_id=0, has_side_effects=True),
        name="gather_all",
    )(tokens, *shards)


class Scatter:
    def __init__(self, bits, grads, outs, locals_, boxes, box_sems, load_sems, send_sems):
        self.bits, self.grads, self.outs, self.locals, self.boxes = bits, grads, outs, locals_, boxes
        self.box_sems, self.load_sems, self.send_sems = box_sems, load_sems, send_sems
        self.orders = [orders_of(bits)[i % 2] for i in range(len(grads))]
        self.me, self.core = lax.axis_index("dp"), lax.axis_index("seq")

    def start(self):
        size = 1 << self.bits
        half = size // 2
        for part in (1, 0):
            for i, grad in enumerate(self.grads):
                masks = masks_of(self.orders[i])
                for place in range(part * half, part * half + half):
                    device = flip_mask(self.me, masks[place])
                    pltpu.make_async_remote_copy(
                        src_ref=grad.at[device * 2 + 1 - self.core], dst_ref=self.boxes[i].at[place],
                        send_sem=self.send_sems.at[i], recv_sem=self.box_sems.at[i, part],
                        device_id=(self.me, 1 - self.core), device_id_type=MESH,
                    ).start()
                    pltpu.make_async_copy(
                        grad.at[device * 2 + self.core], self.locals[i].at[place], self.load_sems.at[i, part]
                    ).start()

    def add(self, i, base, other_ref, other_base, count):
        box = self.boxes[i]

        def one(place, carry):
            total = box[base + place].astype(jnp.float32) + other_ref[other_base + place].astype(jnp.float32)
            box[base + place] = total.astype(jnp.bfloat16)
            return carry

        lax.fori_loop(0, count, one, 0)

    def base(self, step):
        at = 0
        for later in range(self.bits, step, -1):
            at += 1 << later
        return at

    def send(self, i, step):
        count = 1 << step
        pltpu.make_async_remote_copy(
            src_ref=self.boxes[i].at[pl.ds(self.base(step + 1) + count, count)],
            dst_ref=self.boxes[i].at[pl.ds(self.base(step), count)],
            send_sem=self.send_sems.at[i], recv_sem=self.box_sems.at[i, 2 + step],
            device_id=(flip(self.me, 1 << self.orders[i][step]), self.core), device_id_type=MESH,
        ).start()

    def halves(self, part):
        half = 1 << (self.bits - 1)
        for i in range(len(self.grads)):
            wait_bytes(self.locals[i].at[pl.ds(0, half)], self.load_sems.at[i, part])
            wait_bytes(self.boxes[i].at[pl.ds(0, half)], self.box_sems.at[i, part])
            self.add(i, part * half, self.locals[i], part * half, half)
            if part:
                self.send(i, self.bits - 1)

    def step(self, step):
        count = 1 << step
        for i in range(len(self.grads)):
            at, kept = self.base(step), self.base(step + 1)
            wait_bytes(self.boxes[i].at[pl.ds(at, count)], self.box_sems.at[i, 2 + step])
            if step:
                half = count // 2
                self.add(i, at + half, self.boxes[i], kept + half, half)
                self.send(i, step - 1)
                self.add(i, at, self.boxes[i], kept, half)
            else:
                self.outs[i][...] = self.boxes[i][at].astype(jnp.float32) + self.boxes[i][kept].astype(jnp.float32)

    def finish(self):
        total = (2 << self.bits) - 1
        for i in range(len(self.grads)):
            wait_bytes(self.boxes[i].at[pl.ds(0, total)], self.send_sems.at[i])

    def phases(self):
        return (
            [self.start, partial(self.halves, 1), partial(self.halves, 0)]
            + [partial(self.step, step) for step in range(self.bits - 1, -1, -1)]
            + [self.finish]
        )


def scatter_scratch(grads, bits):
    size = 1 << bits
    return (
        [pltpu.VMEM((size,) + grad.shape[1:], jnp.bfloat16) for grad in grads]
        + [pltpu.VMEM((2 * size - 1,) + grad.shape[1:], jnp.bfloat16) for grad in grads]
        + [
            pltpu.SemaphoreType.DMA((len(grads), bits + 2)),
            pltpu.SemaphoreType.DMA((len(grads), 2)),
            pltpu.SemaphoreType.DMA((len(grads),)),
        ]
    )


def scatter_kernel(bits, count, partial_ref, *refs):
    grads, (other_ref, *outs) = refs[:count], refs[count : 2 * count + 1]
    rest = refs[2 * count + 1 :]
    locals_, boxes, sems, swap_sems = rest[:count], rest[count : 2 * count], rest[2 * count : 2 * count + 3], rest[-1]
    me, core = lax.axis_index("dp"), lax.axis_index("seq")
    barrier(bits, me, core)
    scatter = Scatter(bits, grads, outs, locals_, boxes, *sems)
    phases = scatter.phases()
    phases[0]()
    swap = pltpu.make_async_remote_copy(
        src_ref=partial_ref, dst_ref=other_ref, send_sem=swap_sems.at[0], recv_sem=swap_sems.at[1],
        device_id=(me, 1 - core), device_id_type=MESH,
    )
    swap.start()
    for phase in phases[1:]:
        phase()
    swap.wait()


def scatter_all(bits, swapped, grads):
    count = len(grads)
    outs = [jax.ShapeDtypeStruct(swapped.shape, swapped.dtype)]
    outs += [jax.ShapeDtypeStruct(grad.shape[1:], jnp.float32) for grad in grads]
    return pl.pallas_call(
        partial(scatter_kernel, bits, count),
        out_shape=outs,
        in_specs=[ANY] * (count + 1),
        out_specs=[ANY] + [VMEM] * count,
        scratch_shapes=scatter_scratch(grads, bits) + [pltpu.SemaphoreType.DMA((2,))],
        compiler_params=pltpu.CompilerParams(
            collective_id=1, has_side_effects=True, vmem_limit_bytes=58 * 2**20
        ),
        name="scatter_all",
    )(swapped, *grads)


def lane_mask(rows, head):
    lanes = lax.broadcasted_iota(jnp.int32, (rows, PAIR), 1)
    return (lanes // HD) == head


def only(matrix, head):
    return jnp.where(lane_mask(matrix.shape[0], head), matrix, jnp.zeros_like(matrix))


def join_halves(pair_ref, whole_ref, core):
    half = pair_ref.shape[2]
    whole_ref[pl.ds(pl.multiple_of(core * half, half), half)] = pair_ref[0, 0]
    whole_ref[pl.ds(pl.multiple_of((1 - core) * half, half), half)] = pair_ref[1, 0]


def attend_kernel(
    q_ref, k_ref, v_ref, prior_ref, own_ref, all_ref, logits_ref, context_ref, probs_ref, key_ref, value_ref, score_ref
):
    core = lax.axis_index("seq")
    join_halves(k_ref, key_ref, core)
    join_halves(v_ref, value_ref, core)
    rows = q_ref.shape[1]
    chunk = 64
    query = q_ref[0] * jnp.bfloat16(HD ** (-0.5))
    for head in range(2):
        score_ref[head] = cols_product(only(query, head), key_ref[...])
    for start in range(0, rows, chunk):
        same = own_ref[0, pl.ds(start, chunk)] == all_ref[0]
        for head in range(2):
            logits = prior_ref[0, head, pl.ds(start, chunk)].astype(jnp.float32) + score_ref[head, pl.ds(start, chunk)]
            logits_ref[0, head, pl.ds(start, chunk)] = logits.astype(jnp.bfloat16)
            masked = jnp.where(same, logits, mask_fill)
            exponent = jnp.exp(masked - jnp.max(masked, -1, keepdims=True))
            weight = 1.0 / jnp.sum(exponent, -1, keepdims=True)
            probs_ref[0, head, pl.ds(start, chunk)] = (exponent * weight).astype(jnp.bfloat16)
    value = value_ref[...]
    context = matmul(probs_ref[0, 0], only(value, 0)) + matmul(probs_ref[0, 1], only(value, 1))
    context_ref[0] = context.astype(jnp.bfloat16)


def attend(queries, keys, values, prev_logits, own_segment, segment_ids):
    rows, qlength, width = queries.shape
    klength = segment_ids.shape[1]
    rect = pl.BlockSpec((1, 2, qlength, klength), lambda r, p: (r, p, 0, 0))
    slim = pl.BlockSpec((1, qlength, PAIR), lambda r, p: (r, 0, p))
    pair = pl.BlockSpec((2, 1, qlength, PAIR), lambda r, p: (0, r, 0, p))
    return pl.pallas_call(
        attend_kernel,
        grid=(rows, width // PAIR),
        out_shape=[
            jax.ShapeDtypeStruct(prev_logits.shape, jnp.bfloat16),
            jax.ShapeDtypeStruct(queries.shape, jnp.bfloat16),
            jax.ShapeDtypeStruct(prev_logits.shape, jnp.bfloat16),
        ],
        in_specs=[
            slim, pair, pair, rect,
            pl.BlockSpec((1, qlength, 1), lambda r, p: (r, 0, 0)),
            pl.BlockSpec((1, 1, klength), lambda r, p: (r, 0, 0)),
        ],
        out_specs=[rect, slim, rect],
        scratch_shapes=[
            pltpu.VMEM((klength, PAIR), jnp.bfloat16),
            pltpu.VMEM((klength, PAIR), jnp.bfloat16),
            pltpu.VMEM((2, qlength, klength), jnp.float32),
        ],
        compiler_params=pltpu.CompilerParams(vmem_limit_bytes=32 * 2**20),
        name="attend",
    )(queries, keys, values, prev_logits, own_segment[:, :, None], segment_ids[:, None, :])


def attend_back_kernel(
    q_ref, k_ref, v_ref, probs_ref, upstream_ref, context_ref, cotangent_ref,
    logit_grad_ref, query_grad_ref, key_grad_ref, value_grad_ref, key_ref, value_ref, score_ref, turn_ref,
):
    core = lax.axis_index("seq")
    join_halves(k_ref, key_ref, core)
    join_halves(v_ref, value_ref, core)
    rows = q_ref.shape[1]
    chunk = 64
    factor = HD ** (-0.5)
    upstream = upstream_ref[0]
    products = upstream.astype(jnp.float32) * context_ref[0].astype(jnp.float32)
    for head in range(2):
        score_ref[head] = cols_product(only(upstream, head), value_ref[...])
    for head in range(2):
        row_dot = jnp.sum(only(products, head), -1, keepdims=True)
        for start in range(0, rows, chunk):
            span = pl.ds(start, chunk)
            probs = probs_ref[0, head, span].astype(jnp.float32)
            grad = cotangent_ref[0, head, span].astype(jnp.float32) + probs * (
                score_ref[head, span] - row_dot[start : start + chunk]
            )
            logit_grad_ref[0, head, span] = grad.astype(jnp.bfloat16)
    key = key_ref[...]
    query_grad = matmul(logit_grad_ref[0, 0], only(key, 0)) + matmul(logit_grad_ref[0, 1], only(key, 1))
    query_grad_ref[0] = (query_grad * factor).astype(jnp.bfloat16)
    query_turned = (q_ref[0].astype(jnp.float32) * factor).T.astype(jnp.bfloat16)
    upstream_turned = upstream.astype(jnp.float32).T.astype(jnp.bfloat16)
    half = key_grad_ref.shape[2]
    for left, right_ref, out_ref in (
        (query_turned, logit_grad_ref, key_grad_ref),
        (upstream_turned, probs_ref, value_grad_ref),
    ):
        for head in range(2):
            turn_ref[head * HD : (head + 1) * HD] = matmul(left[head * HD : (head + 1) * HD], right_ref[0, head])
        score_ref[0, :, :PAIR] = turn_ref[:, :half].T
        score_ref[1, :, :PAIR] = turn_ref[:, half:].T
        out_ref[0, 0] = score_ref[core, :, :PAIR].astype(jnp.bfloat16)
        out_ref[1, 0] = score_ref[1 - core, :, :PAIR].astype(jnp.bfloat16)


def attend_back(queries, keys, values, probs, upstream, context, cotangent):
    rows, qlength, width = queries.shape
    klength = probs.shape[-1]
    rect = pl.BlockSpec((1, 2, qlength, klength), lambda r, p: (r, p, 0, 0))
    slim = pl.BlockSpec((1, qlength, PAIR), lambda r, p: (r, 0, p))
    pair = pl.BlockSpec((2, 1, qlength, PAIR), lambda r, p: (0, r, 0, p))
    return pl.pallas_call(
        attend_back_kernel,
        grid=(rows, width // PAIR),
        out_shape=[
            jax.ShapeDtypeStruct(cotangent.shape, jnp.bfloat16),
            jax.ShapeDtypeStruct(queries.shape, jnp.bfloat16),
            jax.ShapeDtypeStruct(keys.shape, jnp.bfloat16),
            jax.ShapeDtypeStruct(values.shape, jnp.bfloat16),
        ],
        in_specs=[slim, pair, pair, rect, slim, slim, rect],
        out_specs=[rect, slim, pair, pair],
        scratch_shapes=[
            pltpu.VMEM((klength, PAIR), jnp.bfloat16),
            pltpu.VMEM((klength, PAIR), jnp.bfloat16),
            pltpu.VMEM((2, qlength, klength), jnp.float32),
            pltpu.VMEM((PAIR, klength), jnp.float32),
        ],
        compiler_params=pltpu.CompilerParams(vmem_limit_bytes=32 * 2**20),
        name="attend_back",
    )(queries, keys, values, probs, upstream, context, cotangent)


LANES = 128


def pack_vectors(rows, wide):
    block = jnp.pad(jnp.stack(rows, -2), ((0, 0),) * (rows[0].ndim - 1) + ((0, 0), (0, LANES - rows[0].shape[-1])))
    long_row = jnp.pad(wide, ((0, 0),) * (wide.ndim - 1) + ((0, LANES - wide.shape[-1]),))[..., None, :]
    block = jnp.concatenate([block, long_row], -2)
    return jnp.pad(block, ((0, 0),) * (block.ndim - 2) + ((0, 16 - block.shape[-2]), (0, 0)))


def body(tokens, prev_logits, segment_ids, out_cotangent, logit_cotangent, *shards):
    seqrows, qlength, width = tokens.shape
    slots = seqrows * qlength
    chips = lax.axis_size("dp")
    bits = chips.bit_length() - 1
    devices = 2 * chips
    (
        querymap, querybias, keymap, valuemap, valuebias, mixmap, mixbias, normgain, normbias,
        expandmap, expandbias, shrinkmap, shrinkbias, outgain, outbias,
    ) = shards
    own = querymap.shape[0]
    hidden = expandmap.shape[1]
    wide = expandbias.shape[0]
    own_segment = lax.dynamic_slice_in_dim(segment_ids, lax.axis_index("seq") * qlength, qlength, 1)

    block = pack_vectors(
        [querybias, valuebias, mixbias, normgain, normbias, shrinkbias, outgain, outbias], expandbias
    )
    both_tokens, querymap, keymap, valuemap, block, mixmap, shrinkmap, expandmap = gather_all(
        bits, tokens, [querymap, keymap, valuemap, block, mixmap, shrinkmap, expandmap]
    )
    querymap, keymap, valuemap, mixmap = [m.reshape(width, width) for m in (querymap, keymap, valuemap, mixmap)]
    expandmap = expandmap.reshape(width, hidden)
    shrinkmap = shrinkmap.reshape(hidden, width)
    block = block.astype(jnp.float32)
    rows = block[:, :8, :own].transpose(1, 0, 2).reshape(8, width)
    querybias, valuebias, mixbias, normgain, normbias, shrinkbias, outgain, outbias = [rows[i] for i in range(8)]
    expandbias = block[:, 8, :wide].reshape(hidden)

    token_rows = tokens.reshape(slots, width)
    both_rows = both_tokens.reshape(2 * slots, width)
    queries = (matmul(token_rows, querymap) + querybias).astype(jnp.bfloat16).reshape(seqrows, qlength, width)
    keys = matmul(both_rows, keymap).astype(jnp.bfloat16).reshape(2, seqrows, qlength, width)
    values = (matmul(both_rows, valuemap) + valuebias).astype(jnp.bfloat16).reshape(2, seqrows, qlength, width)
    raw_logits, context_heads, probs = attend(queries, keys, values, prev_logits, own_segment, segment_ids)
    context = context_heads.reshape(slots, width)
    attended = matmul(context, mixmap) + mixbias
    unit_first, scale_first = normalize(token_rows.astype(jnp.float32) + attended)
    normed = (unit_first * normgain + normbias).astype(jnp.bfloat16)
    inner_pre = matmul(normed, expandmap) + expandbias
    active, gelu_slope = jax.jvp(
        partial(jax.nn.gelu, approximate=False), (inner_pre,), (jnp.ones_like(inner_pre),)
    )
    active = active.astype(jnp.bfloat16)
    gelu_slope = gelu_slope.astype(jnp.bfloat16)
    second = normed.astype(jnp.float32) + (matmul(active, shrinkmap) + shrinkbias)
    unit_second, scale_second = normalize(second)
    layer_out = unit_second * outgain + outbias

    upstream = out_cotangent.reshape(slots, width).astype(jnp.float32)
    outgain_grad = jnp.sum(upstream * unit_second, 0)
    outbias_grad = jnp.sum(upstream, 0)
    second_grad = norm_back(upstream, unit_second, scale_second, outgain)
    branch_grad = second_grad.astype(jnp.bfloat16)
    shrinkbias_grad = column_sum(branch_grad)
    shrinkmap_grad = rows_product(active, branch_grad).astype(jnp.bfloat16)
    active_grad = cols_product(branch_grad, shrinkmap)
    inner_grad = (active_grad * gelu_slope.astype(jnp.float32)).astype(jnp.bfloat16)
    expandbias_grad = column_sum(inner_grad)
    expandmap_grad = rows_product(normed, inner_grad).astype(jnp.bfloat16)
    normed_grad = second_grad + cols_product(inner_grad, expandmap)
    normgain_grad = jnp.sum(normed_grad * unit_first, 0)
    normbias_grad = jnp.sum(normed_grad, 0)
    first_grad = norm_back(normed_grad, unit_first, scale_first, normgain)
    attended_grad = first_grad.astype(jnp.bfloat16)
    mixbias_grad = column_sum(attended_grad)
    mixmap_grad = rows_product(context, attended_grad).astype(jnp.bfloat16)
    context_grad = cols_product(attended_grad, mixmap).astype(jnp.bfloat16).reshape(seqrows, qlength, width)
    logits_grad, query_grad, key_grad, value_grad = attend_back(
        queries, keys, values, probs, context_grad, context_heads, logit_cotangent
    )
    query_grad = query_grad.reshape(slots, width)
    key_grad = key_grad.reshape(2 * slots, width)
    value_grad = value_grad.reshape(2 * slots, width)
    other_grad = (
        cols_product(key_grad[slots:], keymap) + cols_product(value_grad[slots:], valuemap)
    ).astype(jnp.bfloat16)
    querymap_grad = rows_product(token_rows, query_grad).astype(jnp.bfloat16)
    querybias_grad = column_sum(query_grad)
    keymap_grad = rows_product(both_rows, key_grad).astype(jnp.bfloat16)
    valuemap_grad = rows_product(both_rows, value_grad).astype(jnp.bfloat16)
    valuebias_grad = column_sum(value_grad)
    tokens_grad = (
        first_grad
        + cols_product(query_grad, querymap)
        + cols_product(key_grad[:slots], keymap)
        + cols_product(value_grad[:slots], valuemap)
    )
    block = pack_vectors(
        [
            grad.reshape(devices, own)
            for grad in (
                querybias_grad, valuebias_grad, mixbias_grad, normgain_grad, normbias_grad,
                shrinkbias_grad, outgain_grad, outbias_grad,
            )
        ],
        expandbias_grad.reshape(devices, wide),
    ).astype(jnp.bfloat16)
    swapped, querymap_grad, keymap_grad, valuemap_grad, block, mixmap_grad, shrinkmap_grad, expandmap_grad = scatter_all(
        bits,
        other_grad,
        [
            querymap_grad.reshape(devices, own, width),
            keymap_grad.reshape(devices, own, width),
            valuemap_grad.reshape(devices, own, width),
            block,
            mixmap_grad.reshape(devices, own, width),
            shrinkmap_grad.reshape(devices, wide, width),
            expandmap_grad.reshape(devices, own, hidden),
        ],
    )
    tokens_grad = tokens_grad + swapped.astype(jnp.float32)
    (
        querybias_grad, valuebias_grad, mixbias_grad, normgain_grad, normbias_grad,
        shrinkbias_grad, outgain_grad, outbias_grad,
    ) = [block[i, :own] for i in range(8)]
    expandbias_grad = block[8, :wide]
    return (
        layer_out.reshape(seqrows, qlength, width).astype(jnp.bfloat16),
        raw_logits,
        tokens_grad.reshape(seqrows, qlength, width).astype(jnp.bfloat16),
        logits_grad,
        querymap_grad, querybias_grad, keymap_grad, valuemap_grad, valuebias_grad,
        mixmap_grad, mixbias_grad, normgain_grad, normbias_grad,
        expandmap_grad, expandbias_grad, shrinkmap_grad, shrinkbias_grad,
        outgain_grad, outbias_grad,
    )


def solution(mesh):
    in_specs = (
        P("dp", "seq", None),
        P("dp", None, "seq", None),
        P("dp", None),
        P("dp", "seq", None),
        P("dp", None, "seq", None),
        P(("dp", "seq"), None),
        P(("dp", "seq")),
        P(("dp", "seq"), None),
        P(("dp", "seq"), None),
        P(("dp", "seq")),
        P(("dp", "seq"), None),
        P(("dp", "seq")),
        P(("dp", "seq")),
        P(("dp", "seq")),
        P(("dp", "seq"), None),
        P(("dp", "seq")),
        P(("dp", "seq"), None),
        P(("dp", "seq")),
        P(("dp", "seq")),
        P(("dp", "seq")),
    )
    out_specs = (
        P("dp", "seq", None),
        P("dp", None, "seq", None),
        P("dp", "seq", None),
        P("dp", None, "seq", None),
        P(("dp", "seq"), None),
        P(("dp", "seq")),
        P(("dp", "seq"), None),
        P(("dp", "seq"), None),
        P(("dp", "seq")),
        P(("dp", "seq"), None),
        P(("dp", "seq")),
        P(("dp", "seq")),
        P(("dp", "seq")),
        P(("dp", "seq"), None),
        P(("dp", "seq")),
        P(("dp", "seq"), None),
        P(("dp", "seq")),
        P(("dp", "seq")),
        P(("dp", "seq")),
    )
    return jax.shard_map(body, mesh=mesh, in_specs=in_specs, out_specs=out_specs, check_vma=False)
```

time: 638 us -> 412 us (0.65)
  waiting for transfers between devices: 297 us -> 0 us
  Pallas kernels: 0 us -> 232 us
  local copies, waits for them, and re-layouts: 123 us -> 45.2 us
  other arithmetic: 60 us -> 19.9 us
  matrix products: 137 us -> 107 us
  between operations: 15 us -> 1.44 us
    pallas_call x0 -> x4, Pallas kernels: none -> 232 us  [the longest x1 96.2 us: scatter_all(): pl.pallas_call(partial(scatter_kernel, bits, count), out_shape=outs, in_s...]
    reduce_scatter x3 -> x0, waiting for transfers between devices: 210 us -> none  [the longest x1 110 us: body(): lax.psum_scatter(jnp.concatenate([querymap_grad.reshape(devices, own, wid...]
    all_gather x3 -> x0, waiting for transfers between devices: 86.9 us -> none  [the longest x2 86.9 us: gather(): return lax.all_gather(block, AXES, axis=0, tiled=False)]
    dot_general x18 -> x0, matrix products: 45 us -> none  [the longest x3 13.8 us: attend(): jnp.einsum('qhe,khe->hqk', query_one, key_one, preferred_element_type=jnp...]
    reshape x15 -> x1, local copies, waits for them, and re-layouts: 30.1 us -> 0.78 us  [body(): expandbias_grad.reshape(devices, wide)]
    sub x6 -> x0, other arithmetic: 29 us -> none  [the longest x3 21.4 us: attend_back(): prob_grad - row_dot]
    slice x15 -> x4, local copies, waits for them, and re-layouts: 31.6 us -> 3.33 us  [the longest x1 1.17 us: body(): value_grad[:slots]]
    while x4 -> x0, local copies, waits for them, and re-layouts: 10.8 us -> none  [the longest x2 6.73 us: body(): lax.map(attend_back, (query_heads, key_heads, value_heads, attention_all,...]
  transfers between devices with their start and end apart: 6 -> 0, of which waited for: 4 -> 0; matrix products, arithmetic and copies ran while one was open for 23% -> 0% of each run, Pallas kernels for 0% -> 0%
where the time goes in v2:
time: 412 us; the launch traced here: 405 us
  Pallas kernels  232 us (56%)
  matrix products  107 us (26%)
  local copies, waits for them, and re-layouts  45.2 us (11%)
  other arithmetic  19.9 us (5%)
    pallas_call x1, Pallas kernels, scatter_all(): pl.pallas_call(partial(scatter_kernel, bits, count), out_shape=outs, in_s...  96.2 us
    pallas_call x1, Pallas kernels, gather_all(): pl.pallas_call(partial(gather_kernel, bits, count), out_shape=outs, in_sp...  93 us
    dot_general x6, matrix products, matmul(): return jnp.dot(left_side, right_side, preferred_element_type=jnp.float32)  50.3 us
    dot_general x8, matrix products, cols_product(): lax.dot_general(left_side, right_side, (((1,), (1,)), ((), ())), preferre...  29.5 us
    dot_general x6, matrix products, rows_product(): lax.dot_general(left_side, right_side, (((0,), (0,)), ((), ())), preferre...  27.3 us
    pallas_call x1, Pallas kernels, attend_back(): pl.pallas_call(attend_back_kernel, grid=(rows, width // PAIR), out_shape=...  22.4 us
    pallas_call x1, Pallas kernels, attend(): pl.pallas_call(attend_kernel, grid=(rows, width // PAIR), out_shape=[jax....  20 us
    unnamed x130, local copies, waits for them, and re-layouts  13.6 us

profile of v2, /device:TPU:0, one launch (start us, length us, event | category | flops | bytes accessed | tf_op | source)
XLA Modules:
  0.0 405.1 jit_solution(6944600122088194683)
XLA Ops:
  2.8 93.0 %gather_all.1 = (bf16[2,3,256,768]{3,2,1,0:T(8,128)(2,1)}, bf16[32,24,768]{2,1,0:T(8,128)(2,1)}, bf16[32,24,768]{2,1,0:T(8,128)(2,1)}, bf16[32,24,768]{2,1,0:T(8...) custom-call(bf16[3,256,768]{2,1,0:T(8,128)(2,1)} %tokens_ref.1, ...), custom_call_target="tpu_custom_call" | custom-call | tf_op jit(solution)/shard_map/gather_all/pallas_call | solution.py:180
  99.9 2.5 add_convert_fusion.6
  102.4 2.0 convolution_convert_fusion.2
  105.8 5.5 %add_convert_fusion.1 = bf16[1536,768]{1,0:T(8,128)(2,1)} fusion(bf16[1536,768]{1,0:T(8,128)(2,1)} %bitcast.165, bf16[768,768]{1,0:T(8,128)(2,1)} %bitcast.137, f32[768]{0:T(1024)} %add.129), kind=kOutput, calls=%fused_computation.20 | convolution fusion | flops 1814298624 | bytes 5901312 | tf_op jit(solution)/shard_map/dot_general | solution.py:23
  117.6 20.0 %attend.1 = (bf16[3,12,256,512]{3,2,1,0:T(8,128)(2,1)}, bf16[3,256,768]{2,1,0:T(8,128)(2,1)S(1)}, bf16[3,12,256,512]{3,2,1,0:T(8,128)(2,1)S(1)}) custom-call(bf16[3,256,768]{2,1,0:T(8,128)(2,1)S(1)} %bitcast.128, bf16[2,3,256,768]{3,2,1,0:T(8,128)(2,1)S(1)} %bitcast.124, bf16[2,3,256,768]{3,2,1,0:T(8,128)(2,1)S(1)} %bitcast.126, ...), custom_call_target="tpu_custom_call" | custom-call | tf_op jit(solution)/shard_map/attend/pallas_call | solution.py:370
  137.6 4.3 %fusion.25 = (f32[768]{0:T(1024)}, f32[768,768]{1,0:T(8,128)}) fusion(f32[768]{0:T(1024)S(1)} %copy-done.47, bf16[768,768]{1,0:T(8,128)(2,1)S(1)} %bitcast.130, bf16[768,768]{1,0:T(8,128)(2,1)S(1)} %bitcast.172, bf16[768,768]{1,0:T(8,128)(2,1)S(1)} %bitcast.143), kind=kOutput, calls=%fused_computation.97 | convolution fusion | flops 908328192 | bytes 5904384 | tf_op jit(solution)/shard_map/dot_general | solution.py:23
  145.3 2.1 multiply_reduce_fusion.3
  147.5 27.9 %multiply_convert_fusion.1 = (bf16[768,3072]{1,0:T(8,128)(2,1)S(1)}, f32[768,3072]{1,0:T(8,128)}, f32[768,3072]{1,0:T(8,128)}) fusion(f32[3072]{0:T(1024)S(1)} %copy-done.42, bf16[768,3072]{1,0:T(8,128)(2,1)} %bitcast.159, f32[768,768]{1,0:T(8,128)S(1)} %copy-done.13, f32[768]{0:T(1024)S(1)} %copy-done.44, f32[768]{0:T(1024)S(1)} %copy-done.36, ...), kind=kOutput, calls=%fused_computation.4 | convolution fusion | flops 3782541312 | bytes 30695424 | tf_op jit(solution)/shard_map/dot_general | solution.py:23
  175.4 8.1 %fusion.26 = (f32[768]{0:T(1024)S(1)}, f32[768,768]{1,0:T(8,128)S(1)}) fusion(f32[768]{0:T(1024)S(1)} %copy-done.46, bf16[768,3072]{1,0:T(8,128)(2,1)S(1)} %get-tuple-element.83, bf16[3072,768]{1,0:T(8,128)(2,1)} %bitcast.163, f32[768]{0:T(1024)S(1)} %copy-done.44, f32[768]{0:T(1024)S(1)} %copy-done.36, f32[768]{0:T(1024)S(1)} %add_rsqrt_fusion.1, ...), kind=kOutput, calls=%fused_computation.98 | convolution fusion | flops 3629186304 | bytes 14174208 | tf_op jit(solution)/shard_map/dot_general | solution.py:23
  187.5 4.9 %fusion.12 = (bf16[768]{0:T(1024)(128)(2,1)}, f32[768]{0:T(1024)S(1)}, bf16[768,768]{1,0:T(8,128)(2,1)}) fusion(bf16[3,256,768]{2,1,0:T(8,128)(2,1)} %param.23, f32[768,768]{1,0:T(8,128)} %copy-done.10, f32[768]{0:T(1024)S(1)} %add_rsqrt_fusion, f32[768]{0:T(1024)S(1)} %broadcast_multiply_fusion.4, f32[768]{0:T(1024)S(1)} %mul.145, f32[768]{0:T(1024)} %add.149), kind=kLoop, calls=%fused_computation.34 | loop fusion | flops 6486528 | bytes 4735488 | tf_op jit(solution)/shard_map/reduce_sum | solution.py:523
  195.2 3.5 convert_reduce_fusion.1
  198.7 13.5 %fusion.27 = (bf16[3072]{0:T(1024)(128)(2,1)}, bf16[768,3072]{1,0:T(8,128)(2,1)}) fusion(f32[768,3072]{1,0:T(8,128)} %get-tuple-element.100, f32[3072]{0:T(1024)S(1)} %copy-done.43, f32[768,3072]{1,0:T(8,128)} %get-tuple-element.84, bf16[3072,768]{1,0:T(8,128)(2,1)} %bitcast.164, f32[768,768]{1,0:T(8,128)S(1)} %get-tuple-element.80), kind=kOutput, calls=%fused_computation.99 | convolution fusion | flops 3659854848 | bytes 30689280 | tf_op jit(solution)/shard_map/dot_general | solution.py:33
  212.3 7.2 %multiply_reduce_fusion = (bf16[768]{0:T(1024)(128)(2,1)}, f32[768]{0:T(1024)S(1)}, f32[768]{0:T(1024)S(1)}, bf16[768]{0:T(1024)(128)(2,1)}, f32[768,768]{1,0:T(8,128)S(1)}) fusion(f32[768,768]{1,0:T(8,128)S(1)} %copy-done.14, f32[768]{0:T(1024)S(1)} %copy-done.40, f32[768]{0:T(1024)S(1)} %broadcast_multiply_fusion.5, f32[768]{0:T(1024)S(1)} %copy-done.37, ...), kind=kOutput, calls=%fused_computation.36 | convolution fusion | flops 3629773824 | bytes 16533504 | tf_op jit(solution)/shard_map/dot_general | solution.py:33
  223.8 22.4 %attend_back.1 = (bf16[3,12,256,512]{3,2,1,0:T(8,128)(2,1)}, bf16[3,256,768]{2,1,0:T(8,128)(2,1)S(1)}, bf16[2,3,256,768]{3,2,1,0:T(8,128)(2,1)S(1)}, bf16[2,3,256,768]{3,2,1,0:T(8,128)(2,1)S(1)}) custom-call(bf16[3,256,768]{2,1,0:T(8,128)(2,1)S(1)} %bitcast.129, bf16[2,3,256,768]{3,2,1,0:T(8,128)(2,1)S(1)} %bitcast.125, ...), custom_call_target="tpu_custom_call" | custom-call | tf_op jit(solution)/shard_map/attend_back/pallas_call | solution.py:441
  251.1 2.1 add_convert_fusion.3.partial_ref
  253.2 2.2 bitcast_convert_fusion.2
  255.4 3.1 bitcast_convert_fusion.1
  258.5 3.2 bitcast_convert_fusion
  263.4 2.7 reduce.5
  278.5 3.9 convolution_convert_fusion.3
  282.5 8.4 %convolution_convert_fusion.1 = bf16[3072,768]{1,0:T(8,128)(2,1)} fusion(bf16[768,3072]{1,0:T(8,128)(2,1)} %copy-done.57, f32[768,768]{1,0:T(8,128)S(1)} %copy-done.20), kind=kOutput, calls=%fused_computation.19 | convolution fusion | flops 3626827776 | bytes 11796480 | tf_op jit(solution)/shard_map/dot_general | solution.py:27
  290.9 6.5 %convolution_convert_fusion = bf16[768,3072]{1,0:T(8,128)(2,1)} fusion(bf16[768,3072]{1,0:T(8,128)(2,1)S(1)} %bitcast.175, f32[768,768]{1,0:T(8,128)S(1)} %copy-done.15, f32[768]{0:T(1024)S(1)} %copy-done.45, f32[768]{0:T(1024)S(1)} %copy-done.38, f32[768]{0:T(1024)S(1)} %copy-done.41, f32[768]{0:T(1024)S(1)} %copy-done.35), kind=kOutput, calls=%fused_computation.18 | convolution fusion | flops 3629187072 | bytes 11808768 | tf_op jit(solution)/shard_map/dot_general | solution.py:27
  297.4 96.2 %scatter_all.1 = (bf16[768,768]{1,0:T(8,128)(2,1)}, f32[24,768]{1,0:T(8,128)}, f32[24,768]{1,0:T(8,128)}, f32[24,768]{1,0:T(8,128)}, f32[16,128]{1,0:T(8,128)}, ...) custom-call(bf16[768,768]{1,0:T(8,128)(2,1)} %add_convert_fusion.3.partial_ref, ...), custom_call_target="tpu_custom_call" | custom-call | tf_op jit(solution)/shard_map/scatter_all/pallas_call | solution.py:311
  397.6 2.2 add_convert_fusion.2
  (187 shorter events, 56.5 us)
Async XLA Ops:
  0.7 99.2 %copy-start.24 = (bf16[3,256,768]{2,1,0:T(8,128)(2,1)S(1)}, bf16[3,256,768]{2,1,0:T(8,128)(2,1)}, u32[]{:S(2)}) copy-start(bf16[3,256,768]{2,1,0:T(8,128)(2,1)} %tokens_ref.1) | copy-start | bytes 3538948
  117.6 20.0 %copy-start.25 = (bf16[3,256,768]{2,1,0:T(8,128)(2,1)S(1)}, bf16[3,256,768]{2,1,0:T(8,128)(2,1)}, u32[]{:S(2)}) copy-start(bf16[3,256,768]{2,1,0:T(8,128)(2,1)} %tokens_ref.1) | copy-start | bytes 3538948
  117.6 20.0 %copy-start.47 = (f32[768]{0:T(1024)S(1)}, f32[768]{0:T(1024)}, u32[]{:S(2)}) copy-start(f32[768]{0:T(1024)} %add.133) | copy-start | bytes 9220
  117.6 20.0 %copy-start.55 = (bf16[32,24,768]{2,1,0:T(8,128)(2,1)S(1)}, bf16[32,24,768]{2,1,0:T(8,128)(2,1)}, u32[]{:S(2)}) copy-start(bf16[32,24,768]{2,1,0:T(8,128)(2,1)} %get-tuple-element.48) | copy-start | bytes 3538948
  145.3 74.1 %copy-start.34 = (f32[768]{0:T(1024)}, f32[768]{0:T(1024)S(1)}, u32[]{:S(2)}) copy-start(f32[768]{0:T(1024)S(1)} %broadcast_multiply_fusion.5) | copy-start | bytes 9220
  147.4 27.9 %copy-start.39 = (f32[768]{0:T(1024)}, f32[768]{0:T(1024)S(1)}, u32[]{:S(2)}) copy-start(f32[768]{0:T(1024)S(1)} %add_rsqrt_fusion.1) | copy-start | bytes 9220
  147.5 27.9 %copy-start.46 = (f32[768]{0:T(1024)S(1)}, f32[768]{0:T(1024)}, u32[]{:S(2)}) copy-start(f32[768]{0:T(1024)} %add.144) | copy-start | bytes 9220
  195.2 17.1 %slice-start = ((s8[4718592]{0:T(1024)(128)(4,1)}), s8[4194304]{0:T(1024)(128)(4,1)S(1)}, s32[]{:S(2)}) async-start(s8[4718592]{0:T(1024)(128)(4,1)} %bitcast.160), calls=%async_computation | async-start | bytes 8388608
  198.7 13.5 %copy-start.19 = (f32[768,768]{1,0:T(8,128)}, f32[768,768]{1,0:T(8,128)S(1)}, u32[]{:S(2)}) copy-start(f32[768,768]{1,0:T(8,128)S(1)} %get-tuple-element.80) | copy-start | bytes 7077892
  198.7 13.5 %copy-start.14 = (f32[768,768]{1,0:T(8,128)S(1)}, f32[768,768]{1,0:T(8,128)}, u32[]{:S(2)}) copy-start(f32[768,768]{1,0:T(8,128)} %get-tuple-element.99) | copy-start | bytes 7077892
  198.7 13.5 %copy-start.37 = (f32[768]{0:T(1024)S(1)}, f32[768]{0:T(1024)}, u32[]{:S(2)}) copy-start(f32[768]{0:T(1024)} %mul.135) | copy-start | bytes 9220
  198.7 13.5 %copy-start.40 = (f32[768]{0:T(1024)S(1)}, f32[768]{0:T(1024)}, u32[]{:S(2)}) copy-start(f32[768]{0:T(1024)} %copy-done.39) | copy-start | bytes 9220
  198.7 13.5 %slice-start.1 = ((s8[4718592]{0:T(1024)(128)(4,1)}), s8[524288]{0:T(1024)(128)(4,1)S(1)}, s32[]{:S(2)}) async-start(s8[4718592]{0:T(1024)(128)(4,1)} %bitcast.160), calls=%async_computation.1 | async-start | bytes 1048576
  246.1 12.4 %copy-start.3 = (bf16[2,3,256,768]{3,2,1,0:T(8,128)(2,1)}, bf16[2,3,256,768]{3,2,1,0:T(8,128)(2,1)S(1)}, u32[]{:S(2)}) copy-start(bf16[2,3,256,768]{3,2,1,0:T(8,128)(2,1)S(1)} %get-tuple-element.55) | copy-start | bytes 7077892
  261.7 12.7 %copy-start.12 = (bf16[3,256,768]{2,1,0:T(8,128)(2,1)S(1)}, bf16[3,256,768]{2,1,0:T(8,128)(2,1)}, u32[]{:S(2)}) copy-start(bf16[3,256,768]{2,1,0:T(8,128)(2,1)} %param.23) | copy-start | bytes 3538948
  262.5 16.0 %copy-start.7 = (bf16[3,256,768]{2,1,0:T(8,128)(2,1)S(1)}, bf16[3,256,768]{2,1,0:T(8,128)(2,1)}, u32[]{:S(2)}) copy-start(bf16[3,256,768]{2,1,0:T(8,128)(2,1)} %copy-done.5) | copy-start | bytes 3538948
  278.5 12.4 %slice-start.2 = ((s8[4718592]{0:T(1024)(128)(4,1)}), s8[4194304]{0:T(1024)(128)(4,1)S(1)}, s32[]{:S(2)}) async-start(s8[4718592]{0:T(1024)(128)(4,1)} %bitcast.174), calls=%async_computation.2 | async-start | bytes 8388608
  282.4 8.4 %copy-start.35 = (f32[768]{0:T(1024)S(1)}, f32[768]{0:T(1024)}, u32[]{:S(2)}) copy-start(f32[768]{0:T(1024)} %copy-done.34) | copy-start | bytes 9220
  282.4 8.4 %copy-start.38 = (f32[768]{0:T(1024)S(1)}, f32[768]{0:T(1024)}, u32[]{:S(2)}) copy-start(f32[768]{0:T(1024)} %mul.135) | copy-start | bytes 9220
  282.4 8.4 %copy-start.41 = (f32[768]{0:T(1024)S(1)}, f32[768]{0:T(1024)}, u32[]{:S(2)}) copy-start(f32[768]{0:T(1024)} %copy-done.39) | copy-start | bytes 9220
  282.4 8.4 %copy-start.45 = (f32[768]{0:T(1024)S(1)}, f32[768]{0:T(1024)}, u32[]{:S(2)}) copy-start(f32[768]{0:T(1024)} %add.138) | copy-start | bytes 9220
  282.4 8.4 %slice-start.3 = ((s8[4718592]{0:T(1024)(128)(4,1)}), s8[524288]{0:T(1024)(128)(4,1)S(1)}, s32[]{:S(2)}) async-start(s8[4718592]{0:T(1024)(128)(4,1)} %bitcast.174), calls=%async_computation.3 | async-start | bytes 1048576
  297.4 96.2 %copy-start.27 = (bf16[1,3,256,768]{3,2,1,0:T(8,128)(2,1)S(1)}, bf16[1,3,256,768]{3,2,1,0:T(8,128)(2,1)}, u32[]{:S(2)}) copy-start(bf16[1,3,256,768]{3,2,1,0:T(8,128)(2,1)} %get-tuple-element.88) | copy-start | bytes 3538948
  297.4 96.2 %copy-start.54 = (bf16[32,24,768]{2,1,0:T(8,128)(2,1)S(1)}, bf16[32,24,768]{2,1,0:T(8,128)(2,1)}, u32[]{:S(2)}) copy-start(bf16[32,24,768]{2,1,0:T(8,128)(2,1)} %get-tuple-element.45) | copy-start | bytes 3538948
  (38 other events, 127.9 us)

commit v3 on v2

--- a/solution.py
+++ b/solution.py
@@ -94,55 +94,92 @@
     pltpu.make_async_copy(region, region, semaphore).wait()
 
 
+def waves(lanes, last):
+    count = max(i + len(lane) for i, lane in enumerate(lanes))
+    merged = [
+        [lane[at - i] for i, lane in enumerate(lanes) if 0 <= at - i < len(lane)] for at in range(count)
+    ]
+    return merged + [last]
+
+
+def run(wave):
+    for phase in wave:
+        phase()
+
+
 class Gather:
-    def __init__(self, bits, shards, fulls, hop_sems, core_sems, send_sems, own_sems):
-        self.bits, self.shards, self.fulls = bits, shards, fulls
+    def __init__(self, bits, plan, shards, fulls, hop_sems, core_sems, send_sems, own_sems):
+        self.bits, self.plan, self.shards, self.fulls = bits, plan, shards, fulls
         self.hop_sems, self.core_sems = hop_sems, core_sems
         self.send_sems, self.own_sems = send_sems, own_sems
-        self.orders = [orders_of(bits)[i % 2] for i in range(len(shards))]
         self.me, self.core = lax.axis_index("dp"), lax.axis_index("seq")
 
     def slot(self, mask):
         return flip_mask(self.me, mask) * 2 + self.core
 
-    def own(self, i):
-        return pltpu.make_async_copy(self.shards[i], self.fulls[i].at[self.slot(0)], self.own_sems.at[i])
-
-    def send(self, i, mask, device, semaphore):
-        slot = self.slot(mask)
-        source = self.fulls[i].at[slot] if mask else self.shards[i]
+    def own(self, at, chunk):
+        array, first, columns, _ = chunk
+        span = pl.ds(first, columns)
+        return pltpu.make_async_copy(
+            self.shards[array].at[:, span], self.fulls[array].at[self.slot(0), :, span], self.own_sems.at[at]
+        )
+
+    def send(self, at, chunk, mask, device, semaphore):
+        array, first, columns, _ = chunk
+        target = self.fulls[array].at[self.slot(mask), :, pl.ds(first, columns)]
+        source = target if mask else self.shards[array].at[:, pl.ds(first, columns)]
         pltpu.make_async_remote_copy(
-            src_ref=source, dst_ref=self.fulls[i].at[slot], send_sem=self.send_sems.at[i],
+            src_ref=source, dst_ref=target, send_sem=self.send_sems.at[at],
             recv_sem=semaphore, device_id=device, device_id_type=MESH,
         ).start()
 
-    def phase(self, step):
-        for i in range(len(self.shards)):
-            masks = masks_of(self.orders[i])
-            fresh = masks[:1] if step == 0 else masks[1 << (step - 1) : 1 << step]
-            if step == 0:
-                self.own(i).start()
-            else:
-                wait_bytes(self.fulls[i].at[pl.ds(0, len(fresh))], self.hop_sems.at[i, step - 1])
-            if step < self.bits:
-                partner = (flip(self.me, 1 << self.orders[i][step]), self.core)
-                for mask in masks[: 1 << step]:
-                    self.send(i, mask, partner, self.hop_sems.at[i, step])
-            for mask in fresh:
-                self.send(i, mask, (self.me, 1 - self.core), self.core_sems.at[i])
-
-    def finish(self):
+    def region(self, chunk, count):
+        array, first, columns, _ = chunk
+        return self.fulls[array].at[pl.ds(0, count), :, pl.ds(first, columns)]
+
+    def phase(self, at, chunk, step):
+        order = orders_of(self.bits)[chunk[3]]
+        masks = masks_of(order)
+        fresh = masks[:1] if step == 0 else masks[1 << (step - 1) : 1 << step]
+        if step == 0:
+            self.own(at, chunk).start()
+        else:
+            wait_bytes(self.region(chunk, len(fresh)), self.hop_sems.at[at, step - 1])
+        if step < self.bits:
+            partner = (flip(self.me, 1 << order[step]), self.core)
+            for mask in masks[: 1 << step]:
+                self.send(at, chunk, mask, partner, self.hop_sems.at[at, step])
+        for mask in fresh:
+            self.send(at, chunk, mask, (self.me, 1 - self.core), self.core_sems.at[at])
+
+    def finish(self, at, chunk):
         size = 1 << self.bits
-        for i in range(len(self.shards)):
-            wait_bytes(self.fulls[i].at[pl.ds(0, size)], self.core_sems.at[i])
-            wait_bytes(self.fulls[i].at[pl.ds(0, 2 * size - 1)], self.send_sems.at[i])
-            self.own(i).wait()
-
-    def phases(self):
-        return [partial(self.phase, step) for step in range(self.bits + 1)] + [self.finish]
-
-
-def gather_scratch(count, bits):
+        wait_bytes(self.region(chunk, size), self.core_sems.at[at])
+        wait_bytes(self.region(chunk, 2 * size - 1), self.send_sems.at[at])
+        self.own(at, chunk).wait()
+
+    def waves(self):
+        lanes, last, at = [], [], 0
+        for lane in self.plan:
+            numbered = [(at + i, chunk) for i, chunk in enumerate(lane)]
+            at += len(lane)
+            lanes.append(
+                [partial(self.lane_step, numbered, step) for step in range(self.bits + 1)]
+            )
+            last += [partial(self.finish, i, chunk) for i, chunk in numbered]
+        return waves(lanes, last)
+
+    def lane_step(self, numbered, step):
+        for at, chunk in numbered:
+            self.phase(at, chunk, step)
+
+
+def chunks_of(plan):
+    return sum(len(lane) for lane in plan)
+
+
+def gather_scratch(plan, bits):
+    count = chunks_of(plan)
     return [
         pltpu.SemaphoreType.DMA((count, bits)),
         pltpu.SemaphoreType.DMA((count,)),
@@ -151,15 +188,18 @@
     ]
 
 
-def gather_kernel(bits, count, tokens_ref, *refs):
+def gather_outs(bits, shards):
+    return [jax.ShapeDtypeStruct((2 << bits,) + shard.shape, shard.dtype) for shard in shards]
+
+
+def gather_kernel(bits, plan, count, tokens_ref, *refs):
     shards, (both_ref, *fulls) = refs[:count], refs[count : 2 * count + 1]
     sems = refs[2 * count + 1 : 2 * count + 5]
     token_sems = refs[2 * count + 5]
     me, core = lax.axis_index("dp"), lax.axis_index("seq")
     barrier(bits, me, core)
-    gather = Gather(bits, shards, fulls, *sems)
-    phases = gather.phases()
-    phases[0]()
+    steps = Gather(bits, plan, shards, fulls, *sems).waves()
+    run(steps[0])
     mine = pltpu.make_async_copy(tokens_ref, both_ref.at[0], token_sems.at[0])
     other = pltpu.make_async_remote_copy(
         src_ref=tokens_ref, dst_ref=both_ref.at[1], send_sem=token_sems.at[1], recv_sem=token_sems.at[2],
@@ -167,53 +207,51 @@
     )
     mine.start()
     other.start()
-    for phase in phases[1:]:
-        phase()
+    for wave in steps[1:]:
+        run(wave)
     mine.wait()
     other.wait()
 
 
-def gather_all(bits, tokens, shards):
-    count, devices = len(shards), 2 << bits
-    outs = [jax.ShapeDtypeStruct((2,) + tokens.shape, tokens.dtype)]
-    outs += [jax.ShapeDtypeStruct((devices,) + shard.shape, shard.dtype) for shard in shards]
+def gather_first(bits, plan, tokens, shards):
+    count = len(shards)
+    outs = [jax.ShapeDtypeStruct((2,) + tokens.shape, tokens.dtype)] + gather_outs(bits, shards)
     return pl.pallas_call(
-        partial(gather_kernel, bits, count),
+        partial(gather_kernel, bits, plan, count),
         out_shape=outs,
         in_specs=[VMEM] * (count + 1),
         out_specs=[ANY] * (count + 1),
-        scratch_shapes=gather_scratch(count, bits) + [pltpu.SemaphoreType.DMA((3,))],
+        scratch_shapes=gather_scratch(plan, bits) + [pltpu.SemaphoreType.DMA((3,))],
         compiler_params=pltpu.CompilerParams(collective_id=0, has_side_effects=True),
-        name="gather_all",
+        name="gather_first",
     )(tokens, *shards)
 
 
 class Scatter:
-    def __init__(self, bits, grads, outs, locals_, boxes, box_sems, load_sems, send_sems):
-        self.bits, self.grads, self.outs, self.locals, self.boxes = bits, grads, outs, locals_, boxes
+    def __init__(self, bits, plan, grads, outs, locals_, boxes, box_sems, load_sems, send_sems):
+        self.bits, self.plan, self.grads, self.outs, self.locals, self.boxes = bits, plan, grads, outs, locals_, boxes
         self.box_sems, self.load_sems, self.send_sems = box_sems, load_sems, send_sems
-        self.orders = [orders_of(bits)[i % 2] for i in range(len(grads))]
         self.me, self.core = lax.axis_index("dp"), lax.axis_index("seq")
 
-    def start(self):
-        size = 1 << self.bits
-        half = size // 2
+    def start(self, at, chunk):
+        array, first, columns, which = chunk
+        grad, span = self.grads[array], pl.ds(first, columns)
+        half = 1 << (self.bits - 1)
+        masks = masks_of(orders_of(self.bits)[which])
         for part in (1, 0):
-            for i, grad in enumerate(self.grads):
-                masks = masks_of(self.orders[i])
-                for place in range(part * half, part * half + half):
-                    device = flip_mask(self.me, masks[place])
-                    pltpu.make_async_remote_copy(
-                        src_ref=grad.at[device * 2 + 1 - self.core], dst_ref=self.boxes[i].at[place],
-                        send_sem=self.send_sems.at[i], recv_sem=self.box_sems.at[i, part],
-                        device_id=(self.me, 1 - self.core), device_id_type=MESH,
-                    ).start()
-                    pltpu.make_async_copy(
-                        grad.at[device * 2 + self.core], self.locals[i].at[place], self.load_sems.at[i, part]
-                    ).start()
-
-    def add(self, i, base, other_ref, other_base, count):
-        box = self.boxes[i]
+            for place in range(part * half, part * half + half):
+                device = flip_mask(self.me, masks[place])
+                pltpu.make_async_remote_copy(
+                    src_ref=grad.at[device * 2 + 1 - self.core, :, span], dst_ref=self.boxes[at].at[place],
+                    send_sem=self.send_sems.at[at], recv_sem=self.box_sems.at[at, part],
+                    device_id=(self.me, 1 - self.core), device_id_type=MESH,
+                ).start()
+                pltpu.make_async_copy(
+                    grad.at[device * 2 + self.core, :, span], self.locals[at].at[place], self.load_sems.at[at, part]
+                ).start()
+
+    def add(self, at, base, other_ref, other_base, count):
+        box = self.boxes[at]
 
         def one(place, carry):
             total = box[base + place].astype(jnp.float32) + other_ref[other_base + place].astype(jnp.float32)
@@ -228,97 +266,126 @@
             at += 1 << later
         return at
 
-    def send(self, i, step):
+    def send(self, at, chunk, step):
         count = 1 << step
+        place = orders_of(self.bits)[chunk[3]][step]
         pltpu.make_async_remote_copy(
-            src_ref=self.boxes[i].at[pl.ds(self.base(step + 1) + count, count)],
-            dst_ref=self.boxes[i].at[pl.ds(self.base(step), count)],
-            send_sem=self.send_sems.at[i], recv_sem=self.box_sems.at[i, 2 + step],
-            device_id=(flip(self.me, 1 << self.orders[i][step]), self.core), device_id_type=MESH,
+            src_ref=self.boxes[at].at[pl.ds(self.base(step + 1) + count, count)],
+            dst_ref=self.boxes[at].at[pl.ds(self.base(step), count)],
+            send_sem=self.send_sems.at[at], recv_sem=self.box_sems.at[at, 2 + step],
+            device_id=(flip(self.me, 1 << place), self.core), device_id_type=MESH,
         ).start()
 
-    def halves(self, part):
+    def halves(self, at, chunk):
         half = 1 << (self.bits - 1)
-        for i in range(len(self.grads)):
-            wait_bytes(self.locals[i].at[pl.ds(0, half)], self.load_sems.at[i, part])
-            wait_bytes(self.boxes[i].at[pl.ds(0, half)], self.box_sems.at[i, part])
-            self.add(i, part * half, self.locals[i], part * half, half)
+        for part in (1, 0):
+            wait_bytes(self.locals[at].at[pl.ds(0, half)], self.load_sems.at[at, part])
+            wait_bytes(self.boxes[at].at[pl.ds(0, half)], self.box_sems.at[at, part])
+            self.add(at, part * half, self.locals[at], part * half, half)
             if part:
-                self.send(i, self.bits - 1)
-
-    def step(self, step):
+                self.send(at, chunk, self.bits - 1)
+
+    def step(self, at, chunk, step):
         count = 1 << step
-        for i in range(len(self.grads)):
-            at, kept = self.base(step), self.base(step + 1)
-            wait_bytes(self.boxes[i].at[pl.ds(at, count)], self.box_sems.at[i, 2 + step])
-            if step:
-                half = count // 2
-                self.add(i, at + half, self.boxes[i], kept + half, half)
-                self.send(i, step - 1)
-                self.add(i, at, self.boxes[i], kept, half)
+        base, kept = self.base(step), self.base(step + 1)
+        wait_bytes(self.boxes[at].at[pl.ds(base, count)], self.box_sems.at[at, 2 + step])
+        if step:
+            half = count // 2
+            self.add(at, base + half, self.boxes[at], kept + half, half)
+            self.send(at, chunk, step - 1)
+            self.add(at, base, self.boxes[at], kept, half)
+        else:
+            array, first, columns, _ = chunk
+            self.outs[array][:, first : first + columns] = (
+                self.boxes[at][base].astype(jnp.float32) + self.boxes[at][kept].astype(jnp.float32)
+            )
+
+    def finish(self, at):
+        wait_bytes(self.boxes[at].at[pl.ds(0, (2 << self.bits) - 1)], self.send_sems.at[at])
+
+    def lane_step(self, numbered, step):
+        for at, chunk in numbered:
+            if step == 0:
+                self.start(at, chunk)
+            elif step == 1:
+                self.halves(at, chunk)
             else:
-                self.outs[i][...] = self.boxes[i][at].astype(jnp.float32) + self.boxes[i][kept].astype(jnp.float32)
-
-    def finish(self):
-        total = (2 << self.bits) - 1
-        for i in range(len(self.grads)):
-            wait_bytes(self.boxes[i].at[pl.ds(0, total)], self.send_sems.at[i])
-
-    def phases(self):
-        return (
-            [self.start, partial(self.halves, 1), partial(self.halves, 0)]
-            + [partial(self.step, step) for step in range(self.bits - 1, -1, -1)]
-            + [self.finish]
-        )
-
-
-def scatter_scratch(grads, bits):
+                self.step(at, chunk, self.bits + 1 - step)
+
+    def waves(self):
+        lanes, last, at = [], [], 0
+        for lane in self.plan:
+            numbered = [(at + i, chunk) for i, chunk in enumerate(lane)]
+            at += len(lane)
+            lanes.append([partial(self.lane_step, numbered, step) for step in range(self.bits + 2)])
+            last += [partial(self.finish, i) for i, _ in numbered]
+        return waves(lanes, last)
+
+
+def scatter_scratch(plan, grads, bits):
     size = 1 << bits
+    shapes = [(grads[chunk[0]].shape[1], chunk[2]) for lane in plan for chunk in lane]
+    count = len(shapes)
     return (
-        [pltpu.VMEM((size,) + grad.shape[1:], jnp.bfloat16) for grad in grads]
-        + [pltpu.VMEM((2 * size - 1,) + grad.shape[1:], jnp.bfloat16) for grad in grads]
+        [pltpu.VMEM((size,) + shape, jnp.bfloat16) for shape in shapes]
+        + [pltpu.VMEM((2 * size - 1,) + shape, jnp.bfloat16) for shape in shapes]
         + [
-            pltpu.SemaphoreType.DMA((len(grads), bits + 2)),
-            pltpu.SemaphoreType.DMA((len(grads), 2)),
-            pltpu.SemaphoreType.DMA((len(grads),)),
+            pltpu.SemaphoreType.DMA((count, bits + 2)),
+            pltpu.SemaphoreType.DMA((count, 2)),
+            pltpu.SemaphoreType.DMA((count,)),
         ]
     )
 
 
-def scatter_kernel(bits, count, partial_ref, *refs):
+def scatter_of(bits, plan, grads, outs, scratch):
+    count = chunks_of(plan)
+    return Scatter(bits, plan, grads, outs, scratch[:count], scratch[count : 2 * count], *scratch[2 * count :])
+
+
+def scatter_outs(grads):
+    return [jax.ShapeDtypeStruct(grad.shape[1:], jnp.float32) for grad in grads]
+
+
+def scatter_kernel(bits, plan, count, partial_ref, *refs):
     grads, (other_ref, *outs) = refs[:count], refs[count : 2 * count + 1]
-    rest = refs[2 * count + 1 :]
-    locals_, boxes, sems, swap_sems = rest[:count], rest[count : 2 * count], rest[2 * count : 2 * count + 3], rest[-1]
+    scratch, swap_sems = refs[2 * count + 1 : -1], refs[-1]
     me, core = lax.axis_index("dp"), lax.axis_index("seq")
     barrier(bits, me, core)
-    scatter = Scatter(bits, grads, outs, locals_, boxes, *sems)
-    phases = scatter.phases()
-    phases[0]()
+    steps = scatter_of(bits, plan, grads, outs, scratch).waves()
+    run(steps[0])
     swap = pltpu.make_async_remote_copy(
         src_ref=partial_ref, dst_ref=other_ref, send_sem=swap_sems.at[0], recv_sem=swap_sems.at[1],
         device_id=(me, 1 - core), device_id_type=MESH,
     )
     swap.start()
-    for phase in phases[1:]:
-        phase()
+    for wave in steps[1:]:
+        run(wave)
     swap.wait()
 
 
-def scatter_all(bits, swapped, grads):
+def scatter_last(bits, plan, swapped, grads):
     count = len(grads)
-    outs = [jax.ShapeDtypeStruct(swapped.shape, swapped.dtype)]
-    outs += [jax.ShapeDtypeStruct(grad.shape[1:], jnp.float32) for grad in grads]
     return pl.pallas_call(
-        partial(scatter_kernel, bits, count),
-        out_shape=outs,
+        partial(scatter_kernel, bits, plan, count),
+        out_shape=[jax.ShapeDtypeStruct(swapped.shape, swapped.dtype)] + scatter_outs(grads),
         in_specs=[ANY] * (count + 1),
         out_specs=[ANY] + [VMEM] * count,
-        scratch_shapes=scatter_scratch(grads, bits) + [pltpu.SemaphoreType.DMA((2,))],
+        scratch_shapes=scatter_scratch(plan, grads, bits) + [pltpu.SemaphoreType.DMA((2,))],
         compiler_params=pltpu.CompilerParams(
-            collective_id=1, has_side_effects=True, vmem_limit_bytes=58 * 2**20
+            collective_id=1, has_side_effects=True, vmem_limit_bytes=40 * 2**20
         ),
-        name="scatter_all",
+        name="scatter_last",
     )(swapped, *grads)
+
+
+def whole(shape):
+    return pl.BlockSpec(shape, lambda r, p: (0,) * len(shape))
+
+
+def spread(steps, at, count):
+    total = len(steps)
+    for i, wave in enumerate(steps):
+        pl.when(at == (i * (count - 1)) // (total - 1))(partial(run, wave))
 
 
 def lane_mask(rows, head):
@@ -336,10 +403,13 @@
     whole_ref[pl.ds(pl.multiple_of((1 - core) * half, half), half)] = pair_ref[1, 0]
 
 
-def attend_kernel(
-    q_ref, k_ref, v_ref, prior_ref, own_ref, all_ref, logits_ref, context_ref, probs_ref, key_ref, value_ref, score_ref
-):
-    core = lax.axis_index("seq")
+def attend_kernel(bits, plan, count, grid, q_ref, k_ref, v_ref, prior_ref, own_ref, all_ref, *refs):
+    shards, (logits_ref, context_ref, probs_ref) = refs[:count], refs[count : count + 3]
+    fulls, (key_ref, value_ref, score_ref) = refs[count + 3 : 2 * count + 3], refs[2 * count + 3 : 2 * count + 6]
+    me, core = lax.axis_index("dp"), lax.axis_index("seq")
+    at = pl.program_id(0) * grid[1] + pl.program_id(1)
+    pl.when(at == 0)(partial(barrier, bits, me, core))
+    spread(Gather(bits, plan, shards, fulls, *refs[2 * count + 6 :]).waves(), at, grid[0] * grid[1])
     join_halves(k_ref, key_ref, core)
     join_halves(v_ref, value_ref, core)
     rows = q_ref.shape[1]
@@ -361,41 +431,48 @@
     context_ref[0] = context.astype(jnp.bfloat16)
 
 
-def attend(queries, keys, values, prev_logits, own_segment, segment_ids):
+def attend(bits, plan, queries, keys, values, prev_logits, own_segment, segment_ids, shards):
     rows, qlength, width = queries.shape
     klength = segment_ids.shape[1]
     rect = pl.BlockSpec((1, 2, qlength, klength), lambda r, p: (r, p, 0, 0))
     slim = pl.BlockSpec((1, qlength, PAIR), lambda r, p: (r, 0, p))
     pair = pl.BlockSpec((2, 1, qlength, PAIR), lambda r, p: (0, r, 0, p))
+    grid = (rows, width // PAIR)
     return pl.pallas_call(
-        attend_kernel,
-        grid=(rows, width // PAIR),
+        partial(attend_kernel, bits, plan, len(shards), grid),
+        grid=grid,
         out_shape=[
             jax.ShapeDtypeStruct(prev_logits.shape, jnp.bfloat16),
             jax.ShapeDtypeStruct(queries.shape, jnp.bfloat16),
             jax.ShapeDtypeStruct(prev_logits.shape, jnp.bfloat16),
-        ],
+        ] + gather_outs(bits, shards),
         in_specs=[
             slim, pair, pair, rect,
             pl.BlockSpec((1, qlength, 1), lambda r, p: (r, 0, 0)),
             pl.BlockSpec((1, 1, klength), lambda r, p: (r, 0, 0)),
-        ],
-        out_specs=[rect, slim, rect],
+        ] + [whole(shard.shape) for shard in shards],
+        out_specs=[rect, slim, rect] + [ANY] * len(shards),
         scratch_shapes=[
             pltpu.VMEM((klength, PAIR), jnp.bfloat16),
             pltpu.VMEM((klength, PAIR), jnp.bfloat16),
             pltpu.VMEM((2, qlength, klength), jnp.float32),
-        ],
-        compiler_params=pltpu.CompilerParams(vmem_limit_bytes=32 * 2**20),
+        ] + gather_scratch(plan, bits),
+        compiler_params=pltpu.CompilerParams(
+            collective_id=2, has_side_effects=True, vmem_limit_bytes=32 * 2**20
+        ),
         name="attend",
-    )(queries, keys, values, prev_logits, own_segment[:, :, None], segment_ids[:, None, :])
+    )(queries, keys, values, prev_logits, own_segment[:, :, None], segment_ids[:, None, :], *shards)
 
 
 def attend_back_kernel(
-    q_ref, k_ref, v_ref, probs_ref, upstream_ref, context_ref, cotangent_ref,
-    logit_grad_ref, query_grad_ref, key_grad_ref, value_grad_ref, key_ref, value_ref, score_ref, turn_ref,
+    bits, plan, count, grid, q_ref, k_ref, v_ref, probs_ref, upstream_ref, context_ref, cotangent_ref, *refs
 ):
-    core = lax.axis_index("seq")
+    grads, (logit_grad_ref, query_grad_ref, key_grad_ref, value_grad_ref) = refs[:count], refs[count : count + 4]
+    outs, (key_ref, value_ref, score_ref, turn_ref) = refs[count + 4 : 2 * count + 4], refs[2 * count + 4 : 2 * count + 8]
+    me, core = lax.axis_index("dp"), lax.axis_index("seq")
+    at = pl.program_id(0) * grid[1] + pl.program_id(1)
+    pl.when(at == 0)(partial(barrier, bits, me, core))
+    spread(scatter_of(bits, plan, grads, outs, refs[2 * count + 8 :]).waves(), at, grid[0] * grid[1])
     join_halves(k_ref, key_ref, core)
     join_halves(v_ref, value_ref, core)
     rows = q_ref.shape[1]
@@ -432,32 +509,35 @@
         out_ref[1, 0] = score_ref[1 - core, :, :PAIR].astype(jnp.bfloat16)
 
 
-def attend_back(queries, keys, values, probs, upstream, context, cotangent):
+def attend_back(bits, plan, queries, keys, values, probs, upstream, context, cotangent, grads):
     rows, qlength, width = queries.shape
     klength = probs.shape[-1]
     rect = pl.BlockSpec((1, 2, qlength, klength), lambda r, p: (r, p, 0, 0))
     slim = pl.BlockSpec((1, qlength, PAIR), lambda r, p: (r, 0, p))
     pair = pl.BlockSpec((2, 1, qlength, PAIR), lambda r, p: (0, r, 0, p))
+    grid = (rows, width // PAIR)
     return pl.pallas_call(
-        attend_back_kernel,
-        grid=(rows, width // PAIR),
+        partial(attend_back_kernel, bits, plan, len(grads), grid),
+        grid=grid,
         out_shape=[
             jax.ShapeDtypeStruct(cotangent.shape, jnp.bfloat16),
             jax.ShapeDtypeStruct(queries.shape, jnp.bfloat16),
             jax.ShapeDtypeStruct(keys.shape, jnp.bfloat16),
             jax.ShapeDtypeStruct(values.shape, jnp.bfloat16),
-        ],
-        in_specs=[slim, pair, pair, rect, slim, slim, rect],
-        out_specs=[rect, slim, pair, pair],
+        ] + scatter_outs(grads),
+        in_specs=[slim, pair, pair, rect, slim, slim, rect] + [ANY] * len(grads),
+        out_specs=[rect, slim, pair, pair] + [whole(grad.shape[1:]) for grad in grads],
         scratch_shapes=[
             pltpu.VMEM((klength, PAIR), jnp.bfloat16),
             pltpu.VMEM((klength, PAIR), jnp.bfloat16),
             pltpu.VMEM((2, qlength, klength), jnp.float32),
             pltpu.VMEM((PAIR, klength), jnp.float32),
-        ],
-        compiler_params=pltpu.CompilerParams(vmem_limit_bytes=32 * 2**20),
+        ] + scatter_scratch(plan, grads, bits),
+        compiler_params=pltpu.CompilerParams(
+            collective_id=3, has_side_effects=True, vmem_limit_bytes=50 * 2**20
+        ),
         name="attend_back",
-    )(queries, keys, values, probs, upstream, context, cotangent)
+    )(queries, keys, values, probs, upstream, context, cotangent, *grads)
 
 
 LANES = 128
@@ -488,23 +568,38 @@
     block = pack_vectors(
         [querybias, valuebias, mixbias, normgain, normbias, shrinkbias, outgain, outbias], expandbias
     )
-    both_tokens, querymap, keymap, valuemap, block, mixmap, shrinkmap, expandmap = gather_all(
-        bits, tokens, [querymap, keymap, valuemap, block, mixmap, shrinkmap, expandmap]
-    )
-    querymap, keymap, valuemap, mixmap = [m.reshape(width, width) for m in (querymap, keymap, valuemap, mixmap)]
-    expandmap = expandmap.reshape(width, hidden)
-    shrinkmap = shrinkmap.reshape(hidden, width)
-    block = block.astype(jnp.float32)
+    thin, third, part = (width // 2) // LANES * LANES, hidden // 3, width // 3
+    both_tokens, querymap, keymap, valuemap, block = gather_first(
+        bits,
+        [
+            [(0, 0, width, 0), (1, 0, width, 1)],
+            [(2, 0, thin, 0), (2, thin, width - thin, 1), (3, 0, LANES, 0)],
+        ],
+        tokens,
+        [querymap, keymap, valuemap, block],
+    )
+    querymap, keymap, valuemap = [m.reshape(width, width) for m in (querymap, keymap, valuemap)]
     rows = block[:, :8, :own].transpose(1, 0, 2).reshape(8, width)
-    querybias, valuebias, mixbias, normgain, normbias, shrinkbias, outgain, outbias = [rows[i] for i in range(8)]
-    expandbias = block[:, 8, :wide].reshape(hidden)
+    rows, expandbias = lax.optimization_barrier((rows, block[:, 8, :wide].reshape(1, hidden)))
+    querybias, valuebias, mixbias, normgain, normbias, shrinkbias, outgain, outbias = [
+        rows[i : i + 1].astype(jnp.float32) for i in range(8)
+    ]
+    expandbias = expandbias.astype(jnp.float32)
 
     token_rows = tokens.reshape(slots, width)
     both_rows = both_tokens.reshape(2 * slots, width)
     queries = (matmul(token_rows, querymap) + querybias).astype(jnp.bfloat16).reshape(seqrows, qlength, width)
     keys = matmul(both_rows, keymap).astype(jnp.bfloat16).reshape(2, seqrows, qlength, width)
     values = (matmul(both_rows, valuemap) + valuebias).astype(jnp.bfloat16).reshape(2, seqrows, qlength, width)
-    raw_logits, context_heads, probs = attend(queries, keys, values, prev_logits, own_segment, segment_ids)
+    raw_logits, context_heads, probs, mixmap, expandmap, shrinkmap = attend(
+        bits,
+        [[(0, 0, width, 0)]]
+        + [[(1, i * third, third, 0), (2, i * part, part, 1)] for i in range(3)],
+        queries, keys, values, prev_logits, own_segment, segment_ids, [mixmap, expandmap, shrinkmap],
+    )
+    mixmap = mixmap.reshape(width, width)
+    expandmap = expandmap.reshape(width, hidden)
+    shrinkmap = shrinkmap.reshape(hidden, width)
     context = context_heads.reshape(slots, width)
     attended = matmul(context, mixmap) + mixbias
     unit_first, scale_first = normalize(token_rows.astype(jnp.float32) + attended)
@@ -538,8 +633,15 @@
     mixbias_grad = column_sum(attended_grad)
     mixmap_grad = rows_product(context, attended_grad).astype(jnp.bfloat16)
     context_grad = cols_product(attended_grad, mixmap).astype(jnp.bfloat16).reshape(seqrows, qlength, width)
-    logits_grad, query_grad, key_grad, value_grad = attend_back(
-        queries, keys, values, probs, context_grad, context_heads, logit_cotangent
+    logits_grad, query_grad, key_grad, value_grad, mixmap_grad, expandmap_grad, shrinkmap_grad = attend_back(
+        bits,
+        [[(1, i * third, third, 0), (2, i * part, part, 1)] for i in range(3)] + [[(0, 0, width, 0)]],
+        queries, keys, values, probs, context_grad, context_heads, logit_cotangent,
+        [
+            mixmap_grad.reshape(devices, own, width),
+            expandmap_grad.reshape(devices, own, hidden),
+            shrinkmap_grad.reshape(devices, wide, width),
+        ],
     )
     query_grad = query_grad.reshape(slots, width)
     key_grad = key_grad.reshape(2 * slots, width)
@@ -558,27 +660,27 @@
         + cols_product(key_grad[:slots], keymap)
         + cols_product(value_grad[:slots], valuemap)
     )
-    block = pack_vectors(
-        [
-            grad.reshape(devices, own)
-            for grad in (
+    stacked = lax.optimization_barrier(
+        jnp.stack(
+            [
                 querybias_grad, valuebias_grad, mixbias_grad, normgain_grad, normbias_grad,
                 shrinkbias_grad, outgain_grad, outbias_grad,
-            )
+            ]
+        )
+    ).reshape(8, devices, own).transpose(1, 0, 2)
+    block = pack_vectors([stacked[:, i] for i in range(8)], expandbias_grad.reshape(devices, wide)).astype(jnp.bfloat16)
+    swapped, querymap_grad, keymap_grad, valuemap_grad, block = scatter_last(
+        bits,
+        [
+            [(0, 0, width, 0), (1, 0, width, 1)],
+            [(2, 0, thin, 0), (2, thin, width - thin, 1), (3, 0, LANES, 0)],
         ],
-        expandbias_grad.reshape(devices, wide),
-    ).astype(jnp.bfloat16)
-    swapped, querymap_grad, keymap_grad, valuemap_grad, block, mixmap_grad, shrinkmap_grad, expandmap_grad = scatter_all(
-        bits,
         other_grad,
         [
             querymap_grad.reshape(devices, own, width),
             keymap_grad.reshape(devices, own, width),
             valuemap_grad.reshape(devices, own, width),
             block,
-            mixmap_grad.reshape(devices, own, width),
-            shrinkmap_grad.reshape(devices, wide, width),
-            expandmap_grad.reshape(devices, own, hidden),
         ],
     )
     tokens_grad = tokens_grad + swapped.astype(jnp.float32)

time: 412 us -> 366 us (0.89)
  Pallas kernels: 232 us -> 207 us
  matrix products: 107 us -> 92.1 us
  other arithmetic: 19.9 us -> 12.5 us
    pallas_call x4, Pallas kernels: 232 us -> 207 us  [the longest x1 72.1 us: attend_back(): pl.pallas_call(partial(attend_back_kernel, bits, plan, len(grads), grid),...]
    unnamed x130 -> x114, local copies, waits for them, and re-layouts: 13.6 us -> 34.1 us
    another operation x10 -> x1, local copies, waits for them, and re-layouts: 11.8 us -> 0.8 us  [pack_vectors(): jnp.stack(rows, -2)]
    dot_general x6, matrix products: 50.3 us -> 41 us  [matmul(): return jnp.dot(left_side, right_side, preferred_element_type=jnp.float32)]
    add x7 -> x0, local copies, waits for them, and re-layouts: 6.27 us -> none  [the longest x1 1.4 us: body(): matmul(both_rows, valuemap) + valuebias]
where the time goes in v3:
time: 366 us; the launch traced here: 360 us
  Pallas kernels  207 us (57%)
  matrix products  92.1 us (25%)
  local copies, waits for them, and re-layouts  46.4 us (13%)
  other arithmetic  12.5 us (3%)
    pallas_call x1, Pallas kernels, attend_back(): pl.pallas_call(partial(attend_back_kernel, bits, plan, len(grads), grid),...  72.1 us
    pallas_call x1, Pallas kernels, attend(): pl.pallas_call(partial(attend_kernel, bits, plan, len(shards), grid), gri...  67.7 us
    dot_general x6, matrix products, matmul(): return jnp.dot(left_side, right_side, preferred_element_type=jnp.float32)  41 us
    pallas_call x1, Pallas kernels, gather_first(): pl.pallas_call(partial(gather_kernel, bits, plan, count), out_shape=outs,...  35.3 us
    unnamed x114, local copies, waits for them, and re-layouts  34.1 us
    pallas_call x1, Pallas kernels, scatter_last(): pl.pallas_call(partial(scatter_kernel, bits, plan, count), out_shape=[jax...  32.2 us
    dot_general x8, matrix products, cols_product(): lax.dot_general(left_side, right_side, (((1,), (1,)), ((), ())), preferre...  25.8 us
    dot_general x6, matrix products, rows_product(): lax.dot_general(left_side, right_side, (((0,), (0,)), ((), ())), preferre...  25.3 us

profile of v3, /device:TPU:0, one launch (start us, length us, event | category | flops | bytes accessed | tf_op | source)
XLA Modules:
  0.0 360.0 jit_solution(16774061985805186543)
XLA Ops:
  2.7 35.3 %gather_first.1 = (bf16[2,3,256,768]{3,2,1,0:T(8,128)(2,1)}, bf16[32,24,768]{2,1,0:T(8,128)(2,1)}, bf16[32,24,768]{2,1,0:T(8,128)(2,1)}, bf16[32,24,768]{2,1,0:T(8,128)(2,1)}, bf16[32,16,128]{2,1,0:T(8,128)(2,1)}) custom-call(bf16[3,256,768]{2,1,0:T(8,128)(2,1)} %tokens_ref.1, bf16[24,768]{1,0:T(8,128)(2,1)} %refs_0_.2, bf16[24,768]{1,0:T(8,128)(2,1)} %refs_1_.2, ...), custom_call_target="tpu_custom_call" | custom-call | tf_op jit(solution)/shard_map/gather_first/pallas_call | solution.py:219
  40.7 4.1 %add_convert_fusion.1 = bf16[1536,768]{1,0:T(8,128)(2,1)S(1)} fusion(bf16[1536,768]{1,0:T(8,128)(2,1)} %bitcast.176, bf16[768,768]{1,0:T(8,128)(2,1)} %bitcast.153, f32[768]{0:T(1024)S(1)} %get-tuple-element.83), kind=kOutput, calls=%fused_computation.21 | convolution fusion | flops 1814298624 | bytes 5901312 | tf_op jit(solution)/shard_map/dot_general | solution.py:23
  47.7 3.5 convolution_convert_fusion.2
  52.5 1.6 copy.43.own_ref
  54.8 1.7 copy-done.1
  60.0 67.7 %attend.1 = (bf16[3,12,256,512]{3,2,1,0:T(8,128)(2,1)}, bf16[3,256,768]{2,1,0:T(8,128)(2,1)S(1)}, bf16[3,12,256,512]{3,2,1,0:T(8,128)(2,1)}, bf16[32,24,768]{2,1...) custom-call(bf16[3,256,768]{2,1,0:T(8,128)(2,1)S(1)} %bitcast.132, ...), custom_call_target="tpu_custom_call" | custom-call | tf_op jit(solution)/shard_map/attend/pallas_call | solution.py:441
  130.7 27.0 %multiply_convert_fusion.1 = (bf16[768,3072]{1,0:T(8,128)(2,1)S(1)}, f32[768,3072]{1,0:T(8,128)}, f32[768,3072]{1,0:T(8,128)}) fusion(f32[3072]{0:T(1024)S(1)} %bitcast.166, bf16[768,3072]{1,0:T(8,128)(2,1)S(1)} %bitcast.140, f32[768,768]{1,0:T(8,128)S(1)} %get-tuple-element.105, f32[768]{0:T(1024)S(1)} %copy-done.37, f32[768]{0:T(1024)S(1)} %copy-done.27, ...), kind=kOutput, calls=%fused_computation.4 | convolution fusion | flops 3782541312 | bytes 30695424 | tf_op jit(solution)/shard_map/dot_general | solution.py:23
  157.8 4.1 %fusion.26 = (f32[768]{0:T(1024)S(1)}, f32[768,768]{1,0:T(8,128)S(1)}) fusion(f32[768]{0:T(1024)S(1)} %copy-done.39, bf16[768,3072]{1,0:T(8,128)(2,1)S(1)} %get-tuple-element.89, bf16[3072,768]{1,0:T(8,128)(2,1)S(1)} %bitcast.144, f32[768]{0:T(1024)S(1)} %copy-done.37, f32[768]{0:T(1024)S(1)} %copy-done.27, f32[768]{0:T(1024)S(1)} %add_rsqrt_fusion.1, ...), kind=kOutput, calls=%fused_computation.102 | convolution fusion | flops 3629186304 | bytes 14174208 | tf_op jit(solution)/shard_map/dot_general | solution.py:23
  168.2 4.0 %convert_reduce_fusion.2 = (bf16[768]{0:T(1024)(128)(2,1)}, f32[768,768]{1,0:T(8,128)S(1)}, bf16[768,768]{1,0:T(8,128)(2,1)}) fusion(f32[768]{0:T(1024)} %broadcast_multiply_fusion.3, f32[768,768]{1,0:T(8,128)S(1)} %get-tuple-element.108, f32[768]{0:T(1024)S(1)} %broadcast_multiply_fusion.4, f32[768]{0:T(1024)} %div.31, f32[768]{0:T(1024)S(1)} %get-tuple-element.77, ...), kind=kLoop, calls=%fused_computation.38 | loop fusion | flops 8256768 | bytes 7097856 | tf_op jit(solution)/shard_map/reduce_sum | solution.py:39
  172.2 8.9 %convolution_convert_fusion = bf16[3072,768]{1,0:T(8,128)(2,1)} fusion(bf16[768,3072]{1,0:T(8,128)(2,1)} %copy-done.48, f32[768,768]{1,0:T(8,128)S(1)} %get-tuple-element.86), kind=kOutput, calls=%fused_computation.18 | convolution fusion | flops 3626827776 | bytes 11796480 | tf_op jit(solution)/shard_map/dot_general | solution.py:27
  181.3 12.4 %fusion.27 = (bf16[3072]{0:T(1024)(128)(2,1)S(1)}, bf16[768,3072]{1,0:T(8,128)(2,1)}) fusion(f32[768,3072]{1,0:T(8,128)} %get-tuple-element.106, f32[3072]{0:T(1024)S(1)} %bitcast.167, f32[768,3072]{1,0:T(8,128)} %get-tuple-element.90, bf16[3072,768]{1,0:T(8,128)(2,1)S(1)} %bitcast.147, f32[768,768]{1,0:T(8,128)} %copy-done.18), kind=kOutput, calls=%fused_computation.103 | convolution fusion | flops 3659854848 | bytes 30689280 | tf_op jit(solution)/shard_map/dot_general | solution.py:33
  193.7 8.9 %convolution_convert_fusion.1 = bf16[768,3072]{1,0:T(8,128)(2,1)} fusion(bf16[768,3072]{1,0:T(8,128)(2,1)} %get-tuple-element.111, f32[768,768]{1,0:T(8,128)S(1)} %copy-done.14, f32[768]{0:T(1024)S(1)} %copy-done.38, f32[768]{0:T(1024)S(1)} %copy-done.28, f32[768]{0:T(1024)S(1)} %copy-done.30, f32[768]{0:T(1024)S(1)} %copy-done.26), kind=kOutput, calls=%fused_computation.19 | convolution fusion | flops 3629187072 | bytes 11808768 | tf_op jit(solution)/shard_map/dot_general | solution.py:27
  202.6 4.4 %multiply_reduce_fusion = (bf16[768]{0:T(1024)(128)(2,1)S(1)}, f32[768]{0:T(1024)S(1)}, f32[768]{0:T(1024)S(1)}, bf16[768]{0:T(1024)(128)(2,1)S(1)}, f32[768,768]{1,0:T(8,128)S(1)}) fusion(f32[768,768]{1,0:T(8,128)S(1)} %copy-done.14, f32[768]{0:T(1024)S(1)} %copy-done.30, f32[768]{0:T(1024)S(1)} %copy-done.26, f32[768]{0:T(1024)S(1)} %copy-done.28, ...), kind=kOutput, calls=%fused_computation.39 | convolution fusion | flops 3629773824 | bytes 16533504 | tf_op jit(solution)/shard_map/dot_general | solution.py:33
  208.4 2.2 convolution_convert_fusion.3
  210.5 2.1 convolution_convert_fusion.4
  212.7 72.1 %attend_back.1 = (bf16[3,12,256,512]{3,2,1,0:T(8,128)(2,1)}, bf16[3,256,768]{2,1,0:T(8,128)(2,1)S(1)}, bf16[2,3,256,768]{3,2,1,0:T(8,128)(2,1)}, bf16[2,3,256,76...) custom-call(bf16[3,256,768]{2,1,0:T(8,128)(2,1)S(1)} %bitcast.133, ...), custom_call_target="tpu_custom_call" | custom-call | tf_op jit(solution)/shard_map/attend_back/pallas_call | solution.py:519
  285.1 2.1 convert_reduce_fusion
  287.7 1.9 fusion.24
  295.0 2.1 bitcast_convert_fusion.1
  297.1 2.1 bitcast_convert_fusion
  300.3 32.2 %scatter_last.1 = (bf16[768,768]{1,0:T(8,128)(2,1)S(1)}, f32[24,768]{1,0:T(8,128)S(1)}, f32[24,768]{1,0:T(8,128)S(1)}, f32[24,768]{1,0:T(8,128)S(1)}, f32[16,128]{1,0:T(8,128)S(1)}) custom-call(bf16[768,768]{1,0:T(8,128)(2,1)S(1)} %add_convert_fusion.3.partial_ref, bf16[32,24,768]{2,1,0:T(8,128)(2,1)S(1)} %bitcast.139, bf16[32,24,768]{2,1,0:T(8,128)(2,1)S(1)} %bitcast.137, ...), custom_call_target="tpu_custom_call" | custom-call | tf_op jit(solution)/shard_map/scatter_last/pallas_call | solution.py:368
  335.5 2.3 add_convert_fusion.2
  338.9 8.4 %copy.64 = bf16[3,12,256,512]{3,2,1,0:T(8,128)(2,1)} copy(bf16[3,12,256,512]{3,2,1,0:T(8,128)(2,1)} %get-tuple-element.134) | data formatting | bytes 18874368
  347.3 8.5 %copy.65 = bf16[3,12,256,512]{3,2,1,0:T(8,128)(2,1)} copy(bf16[3,12,256,512]{3,2,1,0:T(8,128)(2,1)} %get-tuple-element.136) | data formatting | bytes 18874368
  (166 shorter events, 38.7 us)
Async XLA Ops:
  40.7 4.2 %copy-start.43 = (bf16[32,24,768]{2,1,0:T(8,128)(2,1)S(1)}, bf16[32,24,768]{2,1,0:T(8,128)(2,1)}, u32[]{:S(2)}) copy-start(bf16[32,24,768]{2,1,0:T(8,128)(2,1)} %get-tuple-element.44) | copy-start | bytes 3538948
  44.9 9.9 %copy-start = (bf16[1536,768]{1,0:T(8,128)(2,1)}, bf16[1536,768]{1,0:T(8,128)(2,1)S(1)}, u32[]{:S(2)}) copy-start(bf16[1536,768]{1,0:T(8,128)(2,1)S(1)} %add_convert_fusion.1) | copy-start | bytes 7077892
  60.0 67.7 %copy-start.23 = (bf16[3,256,768]{2,1,0:T(8,128)(2,1)S(1)}, bf16[3,256,768]{2,1,0:T(8,128)(2,1)}, u32[]{:S(2)}) copy-start(bf16[3,256,768]{2,1,0:T(8,128)(2,1)} %tokens_ref.1) | copy-start | bytes 3538948
  60.0 67.7 %copy-start.40 = (f32[768]{0:T(1024)S(1)}, f32[768]{0:T(1024)}, u32[]{:S(2)}) copy-start(f32[768]{0:T(1024)} %get-tuple-element.82) | copy-start | bytes 9220
  127.8 29.9 %copy-start.9 = (bf16[32,96,768]{2,1,0:T(8,128)(2,1)}, bf16[32,96,768]{2,1,0:T(8,128)(2,1)S(1)}, u32[]{:S(2)}) copy-start(bf16[32,96,768]{2,1,0:T(8,128)(2,1)S(1)} %get-tuple-element.54) | copy-start | bytes 14155780
  129.1 28.6 %copy-start.13 = (f32[768,768]{1,0:T(8,128)}, f32[768,768]{1,0:T(8,128)S(1)}, u32[]{:S(2)}) copy-start(f32[768,768]{1,0:T(8,128)S(1)} %get-tuple-element.105) | copy-start | bytes 7077892
  129.2 28.6 %copy-start.25 = (f32[768]{0:T(1024)}, f32[768]{0:T(1024)S(1)}, u32[]{:S(2)}) copy-start(f32[768]{0:T(1024)S(1)} %broadcast_multiply_fusion.5) | copy-start | bytes 9220
  129.6 28.1 %copy-start.29 = (f32[768]{0:T(1024)}, f32[768]{0:T(1024)S(1)}, u32[]{:S(2)}) copy-start(f32[768]{0:T(1024)S(1)} %add_rsqrt_fusion.1) | copy-start | bytes 9220
  129.6 28.1 %copy-start.32 = (f32[1,3072]{1,0:T(1,128)}, f32[1,3072]{1,0:T(1,128)S(1)}, u32[]{:S(2)}) copy-start(f32[1,3072]{1,0:T(1,128)S(1)} %add.190) | copy-start | bytes 36868
  130.7 27.1 %copy-start.39 = (f32[768]{0:T(1024)S(1)}, f32[768]{0:T(1024)}, u32[]{:S(2)}) copy-start(f32[768]{0:T(1024)} %get-tuple-element.79) | copy-start | bytes 9220
  163.1 5.1 %copy-start.31 = (f32[768]{0:T(1024)S(1)}, f32[768]{0:T(1024)}, u32[]{:S(2)}) copy-start(f32[768]{0:T(1024)} %get-tuple-element.78) | copy-start | bytes 9220
  168.2 12.9 %slice-start.2 = ((s8[4718592]{0:T(1024)(128)(4,1)}), s8[4194304]{0:T(1024)(128)(4,1)S(1)}, s32[]{:S(2)}) async-start(s8[4718592]{0:T(1024)(128)(4,1)} %bitcast.145), calls=%async_computation.2 | async-start | bytes 8388608
  172.2 8.9 %copy-start.18 = (f32[768,768]{1,0:T(8,128)}, f32[768,768]{1,0:T(8,128)S(1)}, u32[]{:S(2)}) copy-start(f32[768,768]{1,0:T(8,128)S(1)} %get-tuple-element.86) | copy-start | bytes 7077892
  172.2 8.9 %slice-start.3 = ((s8[4718592]{0:T(1024)(128)(4,1)}), s8[524288]{0:T(1024)(128)(4,1)S(1)}, s32[]{:S(2)}) async-start(s8[4718592]{0:T(1024)(128)(4,1)} %bitcast.145), calls=%async_computation.3 | async-start | bytes 1048576
  172.2 8.9 %copy-start.33 = (f32[1,3072]{1,0:T(1,128)S(1)}, f32[1,3072]{1,0:T(1,128)}, u32[]{:S(2)}) copy-start(f32[1,3072]{1,0:T(1,128)} %copy-done.32) | copy-start | bytes 36868
  172.2 30.4 %slice-start = ((s8[4718592]{0:T(1024)(128)(4,1)}), s8[4194304]{0:T(1024)(128)(4,1)S(1)}, s32[]{:S(2)}) async-start(s8[4718592]{0:T(1024)(128)(4,1)} %bitcast.141), calls=%async_computation | async-start | bytes 8388608
  181.2 12.4 %copy-start.14 = (f32[768,768]{1,0:T(8,128)S(1)}, f32[768,768]{1,0:T(8,128)}, u32[]{:S(2)}) copy-start(f32[768,768]{1,0:T(8,128)} %copy-done.13) | copy-start | bytes 7077892
  181.2 12.4 %copy-start.26 = (f32[768]{0:T(1024)S(1)}, f32[768]{0:T(1024)}, u32[]{:S(2)}) copy-start(f32[768]{0:T(1024)} %copy-done.25) | copy-start | bytes 9220
  181.2 12.4 %copy-start.28 = (f32[768]{0:T(1024)S(1)}, f32[768]{0:T(1024)}, u32[]{:S(2)}) copy-start(f32[768]{0:T(1024)} %get-tuple-element.81) | copy-start | bytes 9220
  181.2 12.4 %copy-start.30 = (f32[768]{0:T(1024)S(1)}, f32[768]{0:T(1024)}, u32[]{:S(2)}) copy-start(f32[768]{0:T(1024)} %copy-done.29) | copy-start | bytes 9220
  181.2 12.4 %copy-start.38 = (f32[768]{0:T(1024)S(1)}, f32[768]{0:T(1024)}, u32[]{:S(2)}) copy-start(f32[768]{0:T(1024)} %get-tuple-element.80) | copy-start | bytes 9220
  181.3 21.3 %slice-start.1 = ((s8[4718592]{0:T(1024)(128)(4,1)}), s8[524288]{0:T(1024)(128)(4,1)S(1)}, s32[]{:S(2)}) async-start(s8[4718592]{0:T(1024)(128)(4,1)} %bitcast.141), calls=%async_computation.1 | async-start | bytes 1048576
  193.7 8.9 %copy-start.19 = (f32[768,768]{1,0:T(8,128)S(1)}, f32[768,768]{1,0:T(8,128)}, u32[]{:S(2)}) copy-start(f32[768,768]{1,0:T(8,128)} %copy-done.18) | copy-start | bytes 7077892
  193.7 8.9 %copy-start.47 = (bf16[768,3072]{1,0:T(8,128)(2,1)S(1)}, bf16[768,3072]{1,0:T(8,128)(2,1)}, u32[]{:S(2)}) copy-start(bf16[768,3072]{1,0:T(8,128)(2,1)} %get-tuple-element.111) | copy-start | bytes 14155780
  (29 other events, 56.0 us)
